TPU v7x, 512 devices: a whole 4x4x16 slice. The times are simulated.
512 devices in a mesh: row: 16 (over y, z_hi, core), col: 32 (over z_lo, x).
Axes of the slice: x: 4, y: 4, z: 16 (z_hi: 2, z_lo: 8; z = z_hi * 8 + z_lo), core: 2. Of those that a mesh axis runs over, the one named last changes fastest.
Arguments:
- pair_features: bfloat16 [64, 2048, 2048], P(None, 'col', 'row'), may hold values from -6 to 6
- first_block_kernel: bfloat16 [3, 3, 64, 64], replicated, may hold values from -0.25 to 0.25
- first_block_bias: float32 [64], replicated, may hold values from -3 to 3
- second_block_kernel: bfloat16 [3, 3, 64, 64], replicated, may hold values from -0.25 to 0.25
- second_block_bias: float32 [64], replicated, may hold values from -3 to 3
- head_weight: bfloat16 [37, 64], replicated, may hold values from -32 to 32
- head_bias: float32 [37], replicated, may hold values from -4 to 4
- target: int32 [2048, 2048], P('col', 'row'), may hold values from 0 to 36
Outputs:
- feat_grad: float32 [64, 2048, 2048], P(None, 'col', 'row')
All inputs are finite; a program needn't handle non-finite values.
Results may differ from a plain program's by a relative error of at most 0.0055.
The roundings to bfloat16 on the way count: a program that leaves them out, or rounds other values in their place, can miss the bound.
Values may be sent and summed in bfloat16 or wider, within the bound.
A program may use at most 64 MiB of HBM per device.

v0:
```python
import jax
import jax.numpy as jnp
from jax import lax
from jax.sharding import Mesh
from jax.sharding import PartitionSpec as P

DILATION_FIRST = 4
DILATION_SECOND = 8
COL = ("col_0", "col_1")


def split_up(x, dim, peers):
    before, after = (x.shape[:dim], x.shape[dim + 1 :])
    return jnp.moveaxis(x.reshape(*before, peers, -1, *after), dim, 0)


def in_order(pieces, dim):
    pieces = jnp.moveaxis(pieces, 0, dim)
    lengths = pieces.shape
    return pieces.reshape(*lengths[:dim], lengths[dim] * lengths[dim + 1], *lengths[dim + 2 :])


def turned_blocks(pieces, axes, order):
    inside = pieces.shape[1:]
    whole = pieces.reshape(*(lax.axis_size(a) for a in axes), *inside)
    for k in order:
        whole = lax.all_to_all(whole, axes[k], k, k, tiled=True)
    return whole.reshape(-1, *inside)


def exchange_by_axis(x, axes, order, split_dim, concat_dim):
    pieces = split_up(x, split_dim, lax.axis_size(axes))
    return in_order(turned_blocks(pieces, axes, order), concat_dim)


def padded(cells, sides, width):
    for axis, dim in sides:
        count = lax.axis_size(axis)
        ends = count - 1
        head = lax.slice_in_dim(cells, 0, width, axis=dim)
        tail = lax.slice_in_dim(cells, cells.shape[dim] - width, cells.shape[dim], axis=dim)
        cells = jnp.concatenate(
            [
                lax.ppermute(tail, axis, [(i, (i + 1) % count) for i in range(ends)]),
                cells,
                lax.ppermute(head, axis, [((i + 1) % count, i) for i in range(ends)]),
            ],
            axis=dim,
        )
    return cells


def rounded(tensor):
    return lax.optimization_barrier(tensor.astype(jnp.bfloat16))


def activate(pre_act):
    return jnp.where(pre_act > 0, pre_act, jnp.exp(jnp.minimum(pre_act, 0.0)) - 1.0)


def slope(pre_act):
    return jnp.where(pre_act > 0, 1.0, jnp.exp(jnp.minimum(pre_act, 0.0)))


def flipped_kernel(kernel):
    return jnp.transpose(kernel[::-1, ::-1], (0, 1, 3, 2))


def dilated_kernel(source, kernel, spacing, out_first, out_second, start_first, start_second):
    channels = source.shape[0]
    windows = []
    for tap_first in range(3):
        for tap_second in range(3):
            begin_first = start_first + (tap_first - 1) * spacing
            begin_second = start_second + (tap_second - 1) * spacing
            windows.append(
                source[
                    :,
                    begin_first : begin_first + out_first,
                    begin_second : begin_second + out_second,
                ]
            )
    patches = jnp.stack(windows, axis=0).reshape(9 * channels, out_first * out_second)
    weights = jnp.transpose(kernel, (2, 0, 1, 3)).reshape(kernel.shape[2], 9 * channels)
    return jnp.dot(weights, patches, preferred_element_type=jnp.float32).reshape(
        kernel.shape[2], out_first, out_second
    )


def mirror(tile_block, front_section, third_section):
    layers_in, column_count, row_number_count = tile_block.shape
    group_size = row_number_count // column_count
    col_devices = lax.axis_size(COL)
    row_devices = lax.axis_size("row")
    piece_size = column_count * column_count // col_devices
    sectioned = tile_block.reshape(layers_in, column_count, group_size, column_count).transpose(
        0, 2, 1, 3
    )
    sectioned = front_section(sectioned.reshape(layers_in, group_size, col_devices, piece_size))
    sectioned = sectioned.reshape(layers_in, group_size, row_devices, group_size, piece_size)
    sectioned = sectioned.transpose(0, 2, 1, 3, 4).reshape(
        layers_in, col_devices, group_size, piece_size
    )
    sectioned = third_section(sectioned)
    sectioned = sectioned.transpose(0, 1, 3, 2).reshape(
        layers_in, column_count, column_count, group_size
    )
    return sectioned.transpose(0, 2, 3, 1).reshape(layers_in, column_count, row_number_count)


def local(
    pair_features,
    first_block_kernel,
    first_block_bias,
    second_block_kernel,
    second_block_bias,
    head_weight,
    head_bias,
    target,
):
    channels, column_count, row_number_count = pair_features.shape
    bins_count = head_weight.shape[0]
    target_mirror = mirror(
        target[None],
        lambda sectioned: lax.all_to_all(
            lax.all_to_all(sectioned, COL, split_axis=2, concat_axis=2, tiled=True),
            "row",
            split_axis=2,
            concat_axis=2,
            tiled=True,
        ),
        lambda sectioned: exchange_by_axis(sectioned, COL, (0, 1), 1, 1),
    )[0]
    padded_input = padded(pair_features, (("row", 2), (COL, 1)), DILATION_FIRST)
    first_preactivation = (
        pair_features.astype(jnp.float32)
        + dilated_kernel(
            padded_input,
            first_block_kernel,
            DILATION_FIRST,
            column_count,
            row_number_count,
            DILATION_FIRST,
            DILATION_FIRST,
        )
        + first_block_bias[:, None, None]
    )
    first_hidden = rounded(activate(first_preactivation))
    padded_first_hidden = padded(first_hidden, (("row", 2), (COL, 1)), DILATION_SECOND)
    second_preactivation = (
        first_hidden.astype(jnp.float32)
        + dilated_kernel(
            padded_first_hidden,
            second_block_kernel,
            DILATION_SECOND,
            column_count,
            row_number_count,
            DILATION_SECOND,
            DILATION_SECOND,
        )
        + second_block_bias[:, None, None]
    )
    hidden_two = rounded(activate(second_preactivation))
    feat_front = lambda sectioned: lax.all_to_all(
        lax.all_to_all(sectioned, COL, split_axis=2, concat_axis=2, tiled=True),
        "row",
        split_axis=2,
        concat_axis=2,
        tiled=True,
    )
    mirrored = mirror(
        hidden_two,
        feat_front,
        lambda sectioned: lax.all_to_all(sectioned, COL, split_axis=1, concat_axis=1, tiled=True),
    )
    symmetric = rounded(hidden_two.astype(jnp.float32) + mirrored.astype(jnp.float32))
    logits = (
        jnp.dot(head_weight, symmetric.reshape(channels, -1), preferred_element_type=jnp.float32)
        + head_bias[:, None]
    )
    probability = jax.nn.softmax(logits, axis=0)
    bin_ids = jnp.arange(bins_count, dtype=jnp.int32)[:, None]
    grad_bins = rounded(probability - (bin_ids == target.reshape(1, -1)).astype(jnp.float32))
    grad_mirror = rounded(
        probability - (bin_ids == target_mirror.reshape(1, -1)).astype(jnp.float32)
    )
    bins_sum = rounded(grad_bins.astype(jnp.float32) + grad_mirror.astype(jnp.float32))
    grad_two = jnp.dot(head_weight.T, bins_sum, preferred_element_type=jnp.float32).reshape(
        channels, column_count, row_number_count
    )
    second_delta = rounded(grad_two * slope(second_preactivation))
    padded_gradient = padded(second_delta, (("row", 2), (COL, 1)), DILATION_SECOND)
    first_gradient = second_delta.astype(jnp.float32) + dilated_kernel(
        padded_gradient,
        flipped_kernel(second_block_kernel),
        DILATION_SECOND,
        column_count,
        row_number_count,
        DILATION_SECOND,
        DILATION_SECOND,
    )
    first_delta = rounded(first_gradient * slope(first_preactivation))
    padded_delta_map = padded(first_delta, (("row", 2), (COL, 1)), DILATION_FIRST)
    result = first_delta.astype(jnp.float32) + dilated_kernel(
        padded_delta_map,
        flipped_kernel(first_block_kernel),
        DILATION_FIRST,
        column_count,
        row_number_count,
        DILATION_FIRST,
        DILATION_FIRST,
    )
    return result


def solution(mesh):
    split = Mesh(mesh.devices.reshape(mesh.shape["row"], 8, 4), ("row", "col_0", "col_1"))
    placed = (P(None, COL, "row"), P(), P(), P(), P(), P(), P(), P(COL, "row"))
    return jax.shard_map(
        local, mesh=split, in_specs=placed, out_specs=P(None, COL, "row"), check_vma=False
    )
```

profile of v0, /device:TPU:30, one launch (start us, length us, event | category | flops | bytes accessed | tf_op | source)
XLA Modules:
  0.0 488.4 jit_solution(17394736710220444116)
XLA Ops:
  5.1 15.3 %collective-permute-start.1 = (bf16[64,64,4]{1,0,2:T(8,128)(2,1)S(1)}, bf16[64,64,4]{1,0,2:T(8,128)(2,1)S(1)}, u32[]{:S(2)}, u32[]{:S(2)}) collective-permute-start(bf16[64,64,4]{1,0,2:T(8,128)(2,1)S(1)} %copy.180), channel_id=1, source_target_pairs={{32,0},{64,32},{96,64},{128,96},{160,128},{192,160},{224,192},{256... | collective-permute-start | bytes 98312 | tf_op jit(solution)/shard_map/ppermute | solution.py:46
  31.2 5.6 %collective-permute-done.3 = bf16[64,4,136]{2,1,0:T(4,128)(2,1)} collective-permute-done((bf16[64,4,136]{2,1,0:T(4,128)(2,1)}, bf16[64,4,136]{2,1,0:T(4,128)(2,1)}, u32[]{:S(2)}, u32[]{:S(2)}) %collective-permute-start.3) | collective-permute-done | bytes 69664 | tf_op jit(solution)/shard_map/ppermute | solution.py:46
  36.7 4.7 pad_maximum_fusion
  47.8 5.6 %fusion.20 = f32[8,8,64,128]{3,1,2,0:T(8,128)S(1)} fusion(bf16[64,576]{0,1:T(8,128)(2,1)S(1)} %bitcast.282, bf16[72,8,64,128]{3,2,1,0:T(8,128)(2,1)S(1)} %bitcast.287), kind=kOutput, calls=%fused_computation.42 | convolution fusion | flops 603979776 | bytes 11608064 | tf_op jit(solution)/shard_map/dot_general | solution.py:85
  58.3 12.0 %collective-permute-start.4 = (bf16[64,64,8]{1,2,0:T(8,128)(2,1)S(1)}, bf16[64,64,8]{1,2,0:T(8,128)(2,1)}, u32[]{:S(2)}, u32[]{:S(2)}) collective-permute-start(bf16[64,64,8]{1,2,0:T(8,128)(2,1)S(1)} %copy.142), channel_id=1, source_target_pairs={{0,32},{32,64},{64,96},{96,128},{128,160},{160,192},{192,224},{224... | collective-permute-start | bytes 196616 | tf_op jit(solution)/shard_map/ppermute | solution.py:44
  71.3 3.5 collective-permute-start.5
  75.7 11.9 %all-to-all-start.3 = ((s32[1,2,32,128]{3,1,0,2:T(2,128)}), s32[1,2,32,128]{3,1,0,2:T(2,128)}, u32[]{:S(2)}, u32[]{:S(2)}) async-start(s32[1,2,32,128]{3,1,0,2:T(2,128)} %copy.156), calls=%async_computation.3 | async-start | bytes 65536 | tf_op jit(solution)/shard_map/all_to_all | solution.py:126
  99.2 9.1 %all-to-all-start.4 = ((s32[1,2,32,128]{3,1,0,2:T(2,128)}), s32[1,2,32,128]{3,1,0,2:T(2,128)S(1)}, u32[]{:S(2)}, u32[]{:S(2)}) async-start(s32[1,2,32,128]{3,1,0,2:T(2,128)} %all-to-all-done.3), calls=%async_computation.4 | async-start | bytes 65536 | tf_op jit(solution)/shard_map/all_to_all | solution.py:125
  109.1 12.0 %all-to-all-done.4 = s32[1,2,32,128]{3,1,0,2:T(2,128)S(1)} async-done(((s32[1,2,32,128]{3,1,0,2:T(2,128)}), s32[1,2,32,128]{3,1,0,2:T(2,128)S(1)}, u32[]{:S(2)}, u32[]{:S(2)}) %all-to-all-start.4) | async-done | bytes 32800 | tf_op jit(solution)/shard_map/all_to_all | solution.py:125
  121.7 10.1 %all-to-all-start.5 = ((s32[8,4,1,1,2,128]{5,4,1,3,2,0:T(2,128)}), s32[8,4,1,1,2,128]{5,4,1,3,2,0:T(2,128)S(1)}, u32[]{:S(2)}, u32[]{:S(2)}) async-start(s32[8,4,1,1,2,128]{5,4,1,3,2,0:T(2,128)} %bitcast.37), calls=%async_computation.5 | async-start | bytes 65536 | tf_op jit(solution)/shard_map/all_to_all | solution.py:27
  131.9 4.6 pad_maximum_fusion.1
  141.5 5.6 %fusion.23 = f32[8,8,64,128]{3,1,2,0:T(8,128)S(1)} fusion(bf16[64,576]{0,1:T(8,128)(2,1)S(1)} %bitcast.280, bf16[72,8,64,128]{3,2,1,0:T(8,128)(2,1)S(1)} %bitcast.288), kind=kOutput, calls=%fused_computation.43 | convolution fusion | flops 603979776 | bytes 11608064 | tf_op jit(solution)/shard_map/dot_general | solution.py:85
  151.6 3.5 copy.223
  155.1 3.9 reshape.84
  162.3 63.1 %all_to_all.35 = bf16[64,2,32,128]{3,1,0,2:T(2,128)(2,1)} all-to-all(bf16[64,2,32,128]{3,1,0,2:T(2,128)(2,1)} %copy.150), channel_id=1, replica_groups=mesh['row'=16,'col_0'=8,'col_1'=4] {'col_0','col_1'}, dimensions={2} | all-to-all | bytes 2097152 | tf_op jit(solution)/shard_map/all_to_all | solution.py:165
  225.4 6.2 %all-to-all-start.1 = ((bf16[64,2,32,128]{3,1,0,2:T(2,128)(2,1)}), bf16[64,2,32,128]{3,1,0,2:T(2,128)(2,1)}, u32[]{:S(2)}, u32[]{:S(2)}) async-start(bf16[64,2,32,128]{3,1,0,2:T(2,128)(2,1)} %all_to_all.35), calls=%async_computation.1 | async-start | bytes 2097152 | tf_op jit(solution)/shard_map/all_to_all | solution.py:164
  232.3 44.4 %all-to-all-done.1 = bf16[64,2,32,128]{3,1,0,2:T(2,128)(2,1)} async-done(((bf16[64,2,32,128]{3,1,0,2:T(2,128)(2,1)}), bf16[64,2,32,128]{3,1,0,2:T(2,128)(2,1)}, u32[]{:S(2)}, u32[]{:S(2)}) %all-to-all-start.1) | async-done | bytes 1048608 | tf_op jit(solution)/shard_map/all_to_all | solution.py:164
  276.6 9.2 %all-to-all-start.6 = ((s32[8,4,1,1,2,128]{5,4,0,3,2,1:T(2,128)}), s32[8,4,1,1,2,128]{5,4,0,3,2,1:T(2,128)S(1)}, u32[]{:S(2)}, u32[]{:S(2)}) async-start(s32[8,4,1,1,2,128]{5,4,0,3,2,1:T(2,128)} %copy.159), calls=%async_computation.6 | async-start | bytes 65536 | tf_op jit(solution)/shard_map/all_to_all | solution.py:27
  289.2 12.1 %all-to-all-start.2 = ((bf16[64,32,2,128]{3,0,2,1:T(8,128)(2,1)}), bf16[64,32,2,128]{3,0,2,1:T(8,128)(2,1)}, u32[]{:S(2)}, u32[]{:S(2)}) async-start(bf16[64,32,2,128]{3,0,2,1:T(8,128)(2,1)} %bitcast.273), calls=%async_computation.2 | async-start | bytes 2097152 | tf_op jit(solution)/shard_map/all_to_all | solution.py:174
  304.4 46.6 %all-to-all-done.2 = bf16[64,32,2,128]{3,0,2,1:T(8,128)(2,1)} async-done(((bf16[64,32,2,128]{3,0,2,1:T(8,128)(2,1)}), bf16[64,32,2,128]{3,0,2,1:T(8,128)(2,1)}, u32[]{:S(2)}, u32[]{:S(2)}) %all-to-all-start.2) | async-done | bytes 1048608 | tf_op jit(solution)/shard_map/all_to_all | solution.py:174
  355.0 4.3 reshape.99
  359.4 3.8 copy.178
  376.4 13.2 %collective-permute-start.9 = (bf16[64,64,8]{1,2,0:T(8,128)(2,1)}, bf16[64,64,8]{1,2,0:T(8,128)(2,1)}, u32[]{:S(2)}, u32[]{:S(2)}) collective-permute-start(bf16[64,64,8]{1,2,0:T(8,128)(2,1)} %copy.163), channel_id=1, source_target_pairs={{32,0},{64,32},{96,64},{128,96},{160,128},{192,160},{224,192},{256... | collective-permute-start | bytes 196616 | tf_op jit(solution)/shard_map/ppermute | solution.py:46
  397.2 10.9 %collective-permute-start.10 = (bf16[64,8,144]{2,1,0:T(8,128)(2,1)}, bf16[64,8,144]{2,1,0:T(8,128)(2,1)}, u32[]{:S(2)}, u32[]{:S(2)}) collective-permute-start(bf16[64,8,144]{2,1,0:T(8,128)(2,1)} %get-tuple-element.12), channel_id=1, source_target_pairs={{0,1},{1,2},{2,3},{3,4},{4,5},{5,6},{6,7},{7,8},{8,9},{9,10},{10,1... | collective-permute-start | bytes 442376 | tf_op jit(solution)/shard_map/ppermute | solution.py:44
  412.3 6.5 %collective-permute-done.11 = bf16[64,8,144]{2,1,0:T(8,128)(2,1)} collective-permute-done((bf16[64,8,144]{2,1,0:T(8,128)(2,1)}, bf16[64,8,144]{2,1,0:T(8,128)(2,1)}, u32[]{:S(2)}, u32[]{:S(2)}) %collective-permute-start.11) | collective-permute-done | bytes 147488 | tf_op jit(solution)/shard_map/ppermute | solution.py:46
  418.8 5.0 %pad_maximum_fusion.2 = (bf16[64,72,144]{2,1,0:T(8,128)(2,1)S(1)}, bf16[64,72,144]{2,1,0:T(8,128)(2,1)S(1)}) fusion(bf16[64,8,144]{2,1,0:T(8,128)(2,1)} %collective-permute-done.11, bf16[64,64,8]{2,1,0:T(8,128)(2,1)} %copy.165, bf16[64,64,128]{2,1,0:T(8,128)(2,1)S(1)} %fusion.17, bf16[64,64,8]{2,1,0:T(8,128)(2,1)S(1)} %copy.164, ...), kind=kLoop, calls=%fused_computation.22 | loop fusion | flops 10616832 | bytes 4128768 | tf_op jit(solution)/shard_map/concatenate | solution.py:42
  428.8 5.6 %fusion.26 = f32[8,8,64,128]{3,1,2,0:T(8,128)S(1)} fusion(bf16[64,576]{0,1:T(8,128)(2,1)S(1)} %bitcast.283, bf16[72,8,64,128]{3,2,1,0:T(8,128)(2,1)S(1)} %bitcast.289), kind=kOutput, calls=%fused_computation.44 | convolution fusion | flops 603979776 | bytes 11608064 | tf_op jit(solution)/shard_map/dot_general | solution.py:85
  440.6 13.4 %collective-permute-start.13 = (bf16[64,64,4]{1,0,2:T(8,128)(2,1)S(1)}, bf16[64,64,4]{1,0,2:T(8,128)(2,1)S(1)}, u32[]{:S(2)}, u32[]{:S(2)}) collective-permute-start(bf16[64,64,4]{1,0,2:T(8,128)(2,1)S(1)} %copy.169), channel_id=1, source_target_pairs={{32,0},{64,32},{96,64},{128,96},{160,128},{192,160},{224,192},{256... | collective-permute-start | bytes 98312 | tf_op jit(solution)/shard_map/ppermute | solution.py:46
  460.3 3.7 collective-permute-start.15
  465.7 3.9 collective-permute-done.15
  470.6 3.7 pad_maximum_fusion.3
  480.6 5.6 %fusion.29 = f32[8,8,64,128]{3,1,2,0:T(8,128)S(1)} fusion(bf16[64,576]{0,1:T(8,128)(2,1)S(1)} %bitcast.281, bf16[72,8,64,128]{3,2,1,0:T(8,128)(2,1)S(1)} %bitcast.290), kind=kOutput, calls=%fused_computation.45 | convolution fusion | flops 603979776 | bytes 11608064 | tf_op jit(solution)/shard_map/dot_general | solution.py:85
  (161 shorter events, 118.5 us)
Async XLA Ops:
  0.0 365.1 %copy-start = (bf16[37,64]{1,0:T(8,128)(2,1)S(1)}, bf16[37,64]{1,0:T(8,128)(2,1)}, u32[]{:S(2)}) copy-start(bf16[37,64]{1,0:T(8,128)(2,1)} %param.13) | copy-start | bytes 14212
  2.1 20.8 %copy-start.2 = (bf16[64,64,128]{2,1,0:T(8,128)(2,1)S(1)}, bf16[64,64,128]{2,1,0:T(8,128)(2,1)}, u32[]{:S(2)}) copy-start(bf16[64,64,128]{2,1,0:T(8,128)(2,1)} %param.8) | copy-start | bytes 3145732
  2.6 17.8 %collective-permute-start = (bf16[64,64,4]{1,0,2:T(8,128)(2,1)S(1)}, bf16[64,64,4]{1,0,2:T(8,128)(2,1)S(1)}, u32[]{:S(2)}, u32[]{:S(2)}) collective-permute-start(bf16[64,64,4]{1,0,2:T(8,128)(2,1)S(1)} %copy.179), channel_id=1, source_target_pairs={{0,32},{32,64},{64,96},{96,128},{128,160},{160,192},{192,224},{224... | collective-permute-start | bytes 98312 | tf_op jit(solution)/shard_map/ppermute | solution.py:44
  5.1 17.2 %collective-permute-start.1 = (bf16[64,64,4]{1,0,2:T(8,128)(2,1)S(1)}, bf16[64,64,4]{1,0,2:T(8,128)(2,1)S(1)}, u32[]{:S(2)}, u32[]{:S(2)}) collective-permute-start(bf16[64,64,4]{1,0,2:T(8,128)(2,1)S(1)} %copy.180), channel_id=1, source_target_pairs={{32,0},{64,32},{96,64},{128,96},{160,128},{192,160},{224,192},{256... | collective-permute-start | bytes 98312 | tf_op jit(solution)/shard_map/ppermute | solution.py:46
  21.0 8.8 %copy-start.10 = (bf16[3,3,64,64]{3,2,1,0:T(8,128)(2,1)S(1)}, bf16[3,3,64,64]{3,2,1,0:T(8,128)(2,1)}, u32[]{:S(2)}) copy-start(bf16[3,3,64,64]{3,2,1,0:T(8,128)(2,1)} %param.9) | copy-start | bytes 221188
  24.0 7.2 %collective-permute-start.2 = (bf16[64,4,136]{2,1,0:T(4,128)(2,1)}, bf16[64,4,136]{2,1,0:T(4,128)(2,1)}, u32[]{:S(2)}, u32[]{:S(2)}) collective-permute-start(bf16[64,4,136]{2,1,0:T(4,128)(2,1)} %get-tuple-element.20), channel_id=1, source_target_pairs={{0,1},{1,2},{2,3},{3,4},{4,5},{5,6},{6,7},{7,8},{8,9},{9,10},{10,1... | collective-permute-start | bytes 208904 | tf_op jit(solution)/shard_map/ppermute | solution.py:44
  27.5 9.3 %collective-permute-start.3 = (bf16[64,4,136]{2,1,0:T(4,128)(2,1)}, bf16[64,4,136]{2,1,0:T(4,128)(2,1)}, u32[]{:S(2)}, u32[]{:S(2)}) collective-permute-start(bf16[64,4,136]{2,1,0:T(4,128)(2,1)} %get-tuple-element.19), channel_id=1, source_target_pairs={{1,0},{2,1},{3,2},{4,3},{5,4},{6,5},{7,6},{8,7},{9,8},{10,9},{11,1... | collective-permute-start | bytes 208904 | tf_op jit(solution)/shard_map/ppermute | solution.py:46
  54.1 2.6 copy-start.5
  54.9 20.0 %copy-start.13 = (s32[64,128]{1,0:T(8,128)S(1)}, s32[64,128]{1,0:T(8,128)}, u32[]{:S(2)}) copy-start(s32[64,128]{1,0:T(8,128)} %param.15) | copy-start | bytes 98308
  58.3 29.3 %collective-permute-start.4 = (bf16[64,64,8]{1,2,0:T(8,128)(2,1)S(1)}, bf16[64,64,8]{1,2,0:T(8,128)(2,1)}, u32[]{:S(2)}, u32[]{:S(2)}) collective-permute-start(bf16[64,64,8]{1,2,0:T(8,128)(2,1)S(1)} %copy.142), channel_id=1, source_target_pairs={{0,32},{32,64},{64,96},{96,128},{128,160},{160,192},{192,224},{224... | collective-permute-start | bytes 196616 | tf_op jit(solution)/shard_map/ppermute | solution.py:44
  71.3 17.7 %collective-permute-start.5 = (bf16[64,64,8]{1,2,0:T(8,128)(2,1)}, bf16[64,64,8]{1,2,0:T(8,128)(2,1)}, u32[]{:S(2)}, u32[]{:S(2)}) collective-permute-start(bf16[64,64,8]{1,2,0:T(8,128)(2,1)} %copy.143), channel_id=1, source_target_pairs={{32,0},{64,32},{96,64},{128,96},{160,128},{192,160},{224,192},{256... | collective-permute-start | bytes 196616 | tf_op jit(solution)/shard_map/ppermute | solution.py:46
  75.7 23.5 %all-to-all-start.3 = ((s32[1,2,32,128]{3,1,0,2:T(2,128)}), s32[1,2,32,128]{3,1,0,2:T(2,128)}, u32[]{:S(2)}, u32[]{:S(2)}) async-start(s32[1,2,32,128]{3,1,0,2:T(2,128)} %copy.156), calls=%async_computation.3 | async-start | bytes 65536 | tf_op jit(solution)/shard_map/all_to_all | solution.py:126
  89.0 19.3 %copy-start.9 = (bf16[3,3,64,64]{3,2,1,0:T(8,128)(2,1)S(1)}, bf16[3,3,64,64]{3,2,1,0:T(8,128)(2,1)}, u32[]{:S(2)}) copy-start(bf16[3,3,64,64]{3,2,1,0:T(8,128)(2,1)} %param.11) | copy-start | bytes 221188
  93.4 38.5 %collective-permute-start.6 = (bf16[64,8,144]{2,1,0:T(8,128)(2,1)}, bf16[64,8,144]{2,1,0:T(8,128)(2,1)}, u32[]{:S(2)}, u32[]{:S(2)}) collective-permute-start(bf16[64,8,144]{2,1,0:T(8,128)(2,1)} %get-tuple-element.16), channel_id=1, source_target_pairs={{0,1},{1,2},{2,3},{3,4},{4,5},{5,6},{6,7},{7,8},{8,9},{9,10},{10,1... | collective-permute-start | bytes 442376 | tf_op jit(solution)/shard_map/ppermute | solution.py:44
  96.7 35.1 %collective-permute-start.7 = (bf16[64,8,144]{2,1,0:T(8,128)(2,1)}, bf16[64,8,144]{2,1,0:T(8,128)(2,1)}, u32[]{:S(2)}, u32[]{:S(2)}) collective-permute-start(bf16[64,8,144]{2,1,0:T(8,128)(2,1)} %get-tuple-element.15), channel_id=1, source_target_pairs={{1,0},{2,1},{3,2},{4,3},{5,4},{6,5},{7,6},{8,7},{9,8},{10,9},{11,1... | collective-permute-start | bytes 442376 | tf_op jit(solution)/shard_map/ppermute | solution.py:46
  99.2 21.9 %all-to-all-start.4 = ((s32[1,2,32,128]{3,1,0,2:T(2,128)}), s32[1,2,32,128]{3,1,0,2:T(2,128)S(1)}, u32[]{:S(2)}, u32[]{:S(2)}) async-start(s32[1,2,32,128]{3,1,0,2:T(2,128)} %all-to-all-done.3), calls=%async_computation.4 | async-start | bytes 65536 | tf_op jit(solution)/shard_map/all_to_all | solution.py:125
  121.7 40.6 %all-to-all-start.5 = ((s32[8,4,1,1,2,128]{5,4,1,3,2,0:T(2,128)}), s32[8,4,1,1,2,128]{5,4,1,3,2,0:T(2,128)S(1)}, u32[]{:S(2)}, u32[]{:S(2)}) async-start(s32[8,4,1,1,2,128]{5,4,1,3,2,0:T(2,128)} %bitcast.37), calls=%async_computation.5 | async-start | bytes 65536 | tf_op jit(solution)/shard_map/all_to_all | solution.py:27
  147.1 1.8 copy-start.14
  225.4 51.2 %all-to-all-start.1 = ((bf16[64,2,32,128]{3,1,0,2:T(2,128)(2,1)}), bf16[64,2,32,128]{3,1,0,2:T(2,128)(2,1)}, u32[]{:S(2)}, u32[]{:S(2)}) async-start(bf16[64,2,32,128]{3,1,0,2:T(2,128)(2,1)} %all_to_all.35), calls=%async_computation.1 | async-start | bytes 2097152 | tf_op jit(solution)/shard_map/all_to_all | solution.py:164
  276.6 12.6 %all-to-all-start.6 = ((s32[8,4,1,1,2,128]{5,4,0,3,2,1:T(2,128)}), s32[8,4,1,1,2,128]{5,4,0,3,2,1:T(2,128)S(1)}, u32[]{:S(2)}, u32[]{:S(2)}) async-start(s32[8,4,1,1,2,128]{5,4,0,3,2,1:T(2,128)} %copy.159), calls=%async_computation.6 | async-start | bytes 65536 | tf_op jit(solution)/shard_map/all_to_all | solution.py:27
  289.2 61.8 %all-to-all-start.2 = ((bf16[64,32,2,128]{3,0,2,1:T(8,128)(2,1)}), bf16[64,32,2,128]{3,0,2,1:T(8,128)(2,1)}, u32[]{:S(2)}, u32[]{:S(2)}) async-start(bf16[64,32,2,128]{3,0,2,1:T(8,128)(2,1)} %bitcast.273), calls=%async_computation.2 | async-start | bytes 2097152 | tf_op jit(solution)/shard_map/all_to_all | solution.py:174
  363.2 2.0 copy-start.17
  373.4 16.3 %collective-permute-start.8 = (bf16[64,64,8]{1,2,0:T(8,128)(2,1)}, bf16[64,64,8]{1,2,0:T(8,128)(2,1)}, u32[]{:S(2)}, u32[]{:S(2)}) collective-permute-start(bf16[64,64,8]{1,2,0:T(8,128)(2,1)} %copy.162), channel_id=1, source_target_pairs={{0,32},{32,64},{64,96},{96,128},{128,160},{160,192},{192,224},{224... | collective-permute-start | bytes 196616 | tf_op jit(solution)/shard_map/ppermute | solution.py:44
  376.4 16.5 %collective-permute-start.9 = (bf16[64,64,8]{1,2,0:T(8,128)(2,1)}, bf16[64,64,8]{1,2,0:T(8,128)(2,1)}, u32[]{:S(2)}, u32[]{:S(2)}) collective-permute-start(bf16[64,64,8]{1,2,0:T(8,128)(2,1)} %copy.163), channel_id=1, source_target_pairs={{32,0},{64,32},{96,64},{128,96},{160,128},{192,160},{224,192},{256... | collective-permute-start | bytes 196616 | tf_op jit(solution)/shard_map/ppermute | solution.py:46
  397.2 15.1 %collective-permute-start.10 = (bf16[64,8,144]{2,1,0:T(8,128)(2,1)}, bf16[64,8,144]{2,1,0:T(8,128)(2,1)}, u32[]{:S(2)}, u32[]{:S(2)}) collective-permute-start(bf16[64,8,144]{2,1,0:T(8,128)(2,1)} %get-tuple-element.12), channel_id=1, source_target_pairs={{0,1},{1,2},{2,3},{3,4},{4,5},{5,6},{6,7},{7,8},{8,9},{9,10},{10,1... | collective-permute-start | bytes 442376 | tf_op jit(solution)/shard_map/ppermute | solution.py:44
  408.1 10.7 %collective-permute-start.11 = (bf16[64,8,144]{2,1,0:T(8,128)(2,1)}, bf16[64,8,144]{2,1,0:T(8,128)(2,1)}, u32[]{:S(2)}, u32[]{:S(2)}) collective-permute-start(bf16[64,8,144]{2,1,0:T(8,128)(2,1)} %get-tuple-element.11), channel_id=1, source_target_pairs={{1,0},{2,1},{3,2},{4,3},{5,4},{6,5},{7,6},{8,7},{9,8},{10,9},{11,1... | collective-permute-start | bytes 442376 | tf_op jit(solution)/shard_map/ppermute | solution.py:46
  434.4 1.6 copy-start.6
  438.1 16.4 %collective-permute-start.12 = (bf16[64,64,4]{1,0,2:T(8,128)(2,1)S(1)}, bf16[64,64,4]{1,0,2:T(8,128)(2,1)S(1)}, u32[]{:S(2)}, u32[]{:S(2)}) collective-permute-start(bf16[64,64,4]{1,0,2:T(8,128)(2,1)S(1)} %copy.168), channel_id=1, source_target_pairs={{0,32},{32,64},{64,96},{96,128},{128,160},{160,192},{192,224},{224... | collective-permute-start | bytes 98312 | tf_op jit(solution)/shard_map/ppermute | solution.py:44
  440.6 15.4 %collective-permute-start.13 = (bf16[64,64,4]{1,0,2:T(8,128)(2,1)S(1)}, bf16[64,64,4]{1,0,2:T(8,128)(2,1)S(1)}, u32[]{:S(2)}, u32[]{:S(2)}) collective-permute-start(bf16[64,64,4]{1,0,2:T(8,128)(2,1)S(1)} %copy.169), channel_id=1, source_target_pairs={{32,0},{64,32},{96,64},{128,96},{160,128},{192,160},{224,192},{256... | collective-permute-start | bytes 98312 | tf_op jit(solution)/shard_map/ppermute | solution.py:46
  457.5 7.2 %collective-permute-start.14 = (bf16[64,4,136]{2,0,1:T(8,128)(2,1)}, bf16[64,4,136]{2,0,1:T(8,128)(2,1)}, u32[]{:S(2)}, u32[]{:S(2)}) collective-permute-start(bf16[64,4,136]{2,0,1:T(8,128)(2,1)} %copy.172), channel_id=1, source_target_pairs={{0,1},{1,2},{2,3},{3,4},{4,5},{5,6},{6,7},{7,8},{8,9},{9,10},{10,1... | collective-permute-start | bytes 208904 | tf_op jit(solution)/shard_map/ppermute | solution.py:44
  460.3 9.3 %collective-permute-start.15 = (bf16[64,4,136]{2,0,1:T(8,128)(2,1)}, bf16[64,4,136]{2,0,1:T(8,128)(2,1)}, u32[]{:S(2)}, u32[]{:S(2)}) collective-permute-start(bf16[64,4,136]{2,0,1:T(8,128)(2,1)} %copy.176), channel_id=1, source_target_pairs={{1,0},{2,1},{3,2},{4,3},{5,4},{6,5},{7,6},{8,7},{9,8},{10,9},{11,1... | collective-permute-start | bytes 208904 | tf_op jit(solution)/shard_map/ppermute | solution.py:46
  486.2 2.1 copy-start.1
  (8 other events, 9.8 us)
where the time goes:
time: 494 us; the launch traced here: 488 us
  starting transfers between devices  152 us (31%)
  waiting for transfers between devices  128 us (26%)
  local copies, waits for them, and re-layouts  80.5 us (16%)
  blocking collectives  63.1 us (13%)
  other arithmetic  40.1 us (8%)
  matrix products  23.7 us (5%)
    all_to_all x1, blocking collectives, local(): lax.all_to_all(sectioned, COL, split_axis=2, concat_axis=2, tiled=True)  63.1 us
    all_to_all x2, waiting for transfers between devices, local(): lax.all_to_all(lax.all_to_all(sectioned, COL, split_axis=2, concat_axis=2...  56.4 us
    ppermute x8, starting transfers between devices, padded(): lax.ppermute(head, axis, [((i + 1) % count, i) for i in range(ends)])  56.1 us
    all_to_all x1, waiting for transfers between devices, local(): lax.all_to_all(sectioned, COL, split_axis=1, concat_axis=1, tiled=True)  46.6 us
    ppermute x8, starting transfers between devices, padded(): lax.ppermute(tail, axis, [(i, (i + 1) % count) for i in range(ends)])  37.6 us
    concatenate x8, other arithmetic, padded(): jnp.concatenate([lax.ppermute(tail, axis, [(i, (i + 1) % count) for i in...  23.7 us
    dot_general x4, matrix products, dilated_kernel(): jnp.dot(weights, patches, preferred_element_type=jnp.float32)  22.4 us
    ppermute x8, waiting for transfers between devices, padded(): lax.ppermute(head, axis, [((i + 1) % count, i) for i in range(ends)])  19.8 us
  transfers between devices with their start and end apart: 22, of which 15 were waited for; matrix products, arithmetic and copies ran while one was open for 10% of the time, Pallas kernels for 0%

commit v1 on v0

v1 whole, which is shorter than its diff:
```python
import functools

import jax
import jax.numpy as jnp
from jax import lax
from jax.experimental import pallas as pl
from jax.experimental.pallas import tpu as pltpu
from jax.sharding import PartitionSpec as P

D1 = 4
D2 = 8
HALO = D1 + D2
PER = 128 // HALO
MESH = pl.DeviceIdType.MESH
F32, BF16 = jnp.float32, jnp.bfloat16


def kernel(
    rows, cols, x_hbm, w1, w1t, w2, w2t, b1, b2, hw, hwt, hb, target, out,
    xm, xh, hm, hh, dm, dh, em, eh, ybuf, slope1, slope2, hid, turned,
    pack_out, pack_in, mir_out, mir_in, tgt_out, tgt_in, tgt_here, send, recv, local,
):
    r, c = lax.axis_index("row"), lax.axis_index("col")
    tp, ch, tq = out.shape
    half = tp // 2
    ext = tp + 2 * HALO
    blocks = pack_in.shape[2]
    up, down, left, right = c > 0, c < cols - 1, r > 0, r < rows - 1
    at_up, at_down = (r, jnp.maximum(c - 1, 0)), (r, jnp.minimum(c + 1, cols - 1))
    at_left, at_right = (jnp.maximum(r - 1, 0), c), (jnp.minimum(r + 1, rows - 1), c)
    partners = [(c // 2, 2 * r), (c // 2, 2 * r + 1)]
    other = [jnp.logical_or(pr != r, pc != c) for pr, pc in partners]
    mine = c % 2

    load = pltpu.make_async_copy(x_hbm, xm.at[pl.ds(HALO, tp)], local.at[0])
    load.start()

    barrier = pltpu.get_barrier_semaphore()
    friends = [(up, at_up), (down, at_down), (left, at_left), (right, at_right)]
    friends += list(zip(other, partners))
    for there, who in friends:
        @pl.when(there)
        def _(who=who):
            pl.semaphore_signal(barrier, inc=1, device_id=who, device_id_type=MESH)
    pl.semaphore_wait(barrier, sum(there.astype(jnp.int32) for there, _ in friends))

    lane = lax.broadcasted_iota(jnp.int32, (ch, tq), 1)
    low = lane < tq // 2

    def remote(src, dst, k, who, k_there=None):
        return pltpu.make_async_remote_copy(
            src_ref=src, dst_ref=dst, send_sem=send.at[k],
            recv_sem=recv.at[k if k_there is None else k_there],
            device_id=who, device_id_type=MESH,
        )

    whole = target[...].astype(F32)
    whole = jnp.transpose(jnp.concatenate([whole, whole], axis=0))
    low_rows = lax.broadcasted_iota(jnp.int32, (half, tq), 1) < tq // 2
    for h in range(2):
        a = whole[tp * h : tp * h + half]
        b = whole[tp * h + half : tp * (h + 1)]
        tgt_out[h] = jnp.where(low_rows, a, b)
    def swap(src, dst, k):
        outgoing = [
            remote(src.at[h], dst.at[mine], k + h, partners[h], k + mine) for h in range(2)
        ]
        incoming = [remote(src.at[g], dst.at[g], k + g, partners[g]) for g in range(2)]
        for h in range(2):
            @pl.when(other[h])
            def _(h=h):
                outgoing[h].start()

            @pl.when(jnp.logical_not(other[h]))
            def _(h=h):
                dst[h] = src[h]

        def arrive():
            for g in range(2):
                @pl.when(other[g])
                def _(g=g):
                    incoming[g].wait_recv()

        def leave():
            for h in range(2):
                @pl.when(other[h])
                def _(h=h):
                    outgoing[h].wait_send()

        return arrive, leave

    tgt_arrive, tgt_leave = swap(tgt_out, tgt_in, 16)

    def edges(main, halo, which, base):
        first = remote(main.at[pl.ds(HALO, HALO)], main.at[pl.ds(HALO + tp, HALO)], base, at_up)
        last = remote(main.at[pl.ds(tp, HALO)], main.at[pl.ds(0, HALO)], base + 1, at_down)
        parts = [(2, blocks - 4), (0, 2), (blocks - 2, 2)]

        def side(s, n):
            lo, count = parts[n]
            span = pl.ds(lo, count)
            return remote(
                pack_out.at[which, s, span], pack_in.at[which, s, span],
                base + 2 + 3 * s + n, (at_left, at_right)[s],
            )

        @pl.when(up)
        def _():
            first.start()

        @pl.when(down)
        def _():
            last.start()

        def pack(b, carry):
            first_lanes = jnp.zeros((ch, tq), F32)
            last_lanes = jnp.zeros((ch, tq), F32)
            for j in range(PER):
                row = main[b * PER + j].astype(F32)
                slot = jnp.logical_and(lane >= HALO * j, lane < HALO * (j + 1))
                shifted = pltpu.roll(row, HALO * j, 1) if j else row
                first_lanes = jnp.where(slot, shifted, first_lanes)
                last_lanes = jnp.where(
                    slot, pltpu.roll(row, (HALO * (j + 1)) % tq, 1), last_lanes
                )
            pack_out[which, 0, b] = first_lanes.astype(BF16)
            pack_out[which, 1, b] = last_lanes.astype(BF16)
            return carry

        def begin(n):
            @pl.when(left)
            def _():
                side(0, n).start()

            @pl.when(right)
            def _():
                side(1, n).start()

        lax.fori_loop(2, blocks - 2, pack, 0)
        begin(0)

        @pl.when(down)
        def _():
            first.wait_recv()

        @pl.when(jnp.logical_not(down))
        def _():
            main[pl.ds(HALO + tp, HALO)] = jnp.zeros((HALO, ch, tq), BF16)

        @pl.when(up)
        def _():
            last.wait_recv()

        @pl.when(jnp.logical_not(up))
        def _():
            main[pl.ds(0, HALO)] = jnp.zeros((HALO, ch, tq), BF16)

        lax.fori_loop(0, 2, pack, 0)
        begin(1)
        lax.fori_loop(blocks - 2, blocks, pack, 0)
        begin(2)

        for n in range(3):
            @pl.when(right)
            def _(n=n):
                side(0, n).wait_recv()

            @pl.when(left)
            def _(n=n):
                side(1, n).wait_recv()

        for s, there in ((0, right), (1, left)):
            @pl.when(jnp.logical_not(there))
            def _(s=s):
                pack_in[which, s] = jnp.zeros(pack_in.shape[2:], BF16)

        def unpack(b, carry):
            after = pack_in[which, 0, b].astype(F32)
            before = pack_in[which, 1, b].astype(F32)
            for j in range(PER):
                a = pltpu.roll(after, (-HALO * j) % tq, 1) if j else after
                z = pltpu.roll(before, (-HALO * (j + 1)) % tq, 1)
                halo[b * PER + j] = jnp.where(low, a, z).astype(BF16)
            return carry

        lax.fori_loop(0, blocks, unpack, 0)

        def finish():
            @pl.when(up)
            def _():
                first.wait_send()

            @pl.when(down)
            def _():
                last.wait_send()

            for n in range(3):
                @pl.when(left)
                def _(n=n):
                    side(0, n).wait_send()

                @pl.when(right)
                def _(n=n):
                    side(1, n).wait_send()

        return finish

    def taps(main, halo, d, wide):
        lm, lh = pltpu.roll(main, tq - d, 1), pltpu.roll(halo, tq - d, 1)
        rm, rh = pltpu.roll(main, d, 1), pltpu.roll(halo, d, 1)
        head, tail = lane < d, lane >= tq - d
        first = [jnp.where(head, rh, rm), main, jnp.where(tail, lh, lm)]
        first = jnp.concatenate(first, axis=0).astype(BF16)
        if not wide:
            return first
        second = [jnp.where(head, rm, rh), halo, jnp.where(tail, lm, lh)]
        return jnp.concatenate([first, jnp.concatenate(second, axis=0).astype(BF16)], axis=1)

    def conv(weights, patches, count, lag, done):
        w = weights[...]

        def step(j, finish):
            y = jnp.dot(w, patches(j), preferred_element_type=F32)
            ybuf[j] = y[: 2 * ch]
            if finish:
                done(j - 2 * lag, ybuf[j - 2 * lag, :ch] + ybuf[j - lag, ch:] + y[2 * ch :])

        def loop(lo, hi, finish):
            def body(j, carry):
                step(lo + 2 * j, finish)
                step(lo + 2 * j + 1, finish)
                return carry

            lax.fori_loop(0, (hi - lo) // 2, body, 0)

        loop(0, 2 * lag, False)
        loop(2 * lag, count, True)

    def wide_rows(main, halo, d):
        return lambda j: taps(main[j].astype(F32), halo[j].astype(F32), d, True)

    def row_pairs(main, halo, d):
        def patches(j):
            one = taps(main[2 * j].astype(F32), halo[2 * j].astype(F32), d, False)
            two = taps(main[2 * j + 1].astype(F32), halo[2 * j + 1].astype(F32), d, False)
            return jnp.concatenate([one, two], axis=1)

        return patches

    side_ok = jnp.where(low, jnp.where(right, 1.0, 0.0), jnp.where(left, 1.0, 0.0))

    def row_ok(p):
        inside = jnp.logical_and(jnp.logical_or(up, p >= 0), jnp.logical_or(down, p < tp))
        return jnp.where(inside, 1.0, 0.0).astype(F32)

    load.wait()
    pad = blocks * PER - ext
    if pad:
        xm[pl.ds(ext, pad)] = jnp.zeros((pad, ch, tq), BF16)
        dm[pl.ds(ext, pad)] = jnp.zeros((pad, ch, tq), BF16)
    finish_x = edges(xm, xh, 0, 0)
    bias1 = jnp.broadcast_to(b1[...], (ch, tq))
    bias2 = jnp.broadcast_to(b2[...], (ch, tq))

    def first_done(o, total):
        ok = row_ok(o - D2)
        for n, (src, dst) in enumerate(((xm, hm), (xh, hh))):
            pre = src[o + D1].astype(F32) + total[:, tq * n : tq * (n + 1)] + bias1
            e = jnp.exp(jnp.minimum(pre, 0.0))
            slope1[o, :, tq * n : tq * (n + 1)] = jnp.where(pre > 0, 1.0, e)
            act = jnp.where(pre > 0, pre, e - 1.0) * ok
            dst[o] = (act * side_ok if n else act).astype(BF16)

    conv(w1, wide_rows(xm, xh, D1), ext, D1, first_done)

    def second_done(m, total):
        for n in range(2):
            o = 2 * m + n
            pre = hm[o + D2].astype(F32) + total[:, tq * n : tq * (n + 1)] + bias2
            e = jnp.exp(jnp.minimum(pre, 0.0))
            slope2[o] = jnp.where(pre > 0, 1.0, e)
            hid[o] = jnp.where(pre > 0, pre, e - 1.0).astype(BF16).astype(F32)

    conv(w2, row_pairs(hm, hh, D2), (tp + 2 * D2) // 2, D2 // 2, second_done)

    def turn(o, carry):
        plane = hid[:, o, :]
        plane = jnp.transpose(jnp.concatenate([plane, plane], axis=0))
        for h in range(2):
            a = plane[tp * h : tp * h + half]
            b = plane[tp * h + half : tp * (h + 1)]
            turned[pl.ds(half * h, half), o, :] = jnp.where(low_rows, a, b)
        return carry

    lax.fori_loop(0, ch, turn, 0)

    def settle(j, carry):
        mir_out[0, j] = turned[j].astype(BF16)
        mir_out[1, j] = turned[half + j].astype(BF16)
        return carry

    lax.fori_loop(0, half, settle, 0)

    mir_arrive, mir_leave = swap(mir_out, mir_in, 18)
    tgt_arrive()
    mir_arrive()

    weight, weight_t = hw[...], hwt[...]
    bins = weight.shape[0]
    bias = jnp.broadcast_to(hb[...], (bins, 2 * tq))
    bin_ids = lax.broadcasted_iota(jnp.int32, (bins, 2 * tq), 0).astype(F32)
    low_row = lax.broadcasted_iota(jnp.int32, (1, tq), 1) < tq // 2

    def facing(zero, one, mask):
        first = jnp.where(mask, zero, pltpu.roll(one, tq // 2, 1))
        second = jnp.where(mask, pltpu.roll(zero, tq // 2, 1), one)
        return jnp.concatenate([first, second], axis=1)

    tgt_here[...] = target[...].astype(F32)

    def head(j, carry):
        mirrored = facing(mir_in[0, j].astype(F32), mir_in[1, j].astype(F32), low)
        own = jnp.concatenate([hid[j], hid[j + half]], axis=1)
        symmetric = (own + mirrored).astype(BF16)
        logits = jnp.dot(weight, symmetric, preferred_element_type=F32) + bias
        e = jnp.exp(logits - jnp.max(logits, axis=0, keepdims=True))
        probability = e / jnp.sum(e, axis=0, keepdims=True)
        t_own = jnp.concatenate(
            [tgt_here[pl.ds(j, 1), :], tgt_here[pl.ds(j + half, 1), :]], axis=1
        )
        t_mirror = facing(tgt_in[0, pl.ds(j, 1), :], tgt_in[1, pl.ds(j, 1), :], low_row)
        grad = (probability - (bin_ids == t_own).astype(F32)).astype(BF16).astype(F32)
        grad_mirror = (probability - (bin_ids == t_mirror).astype(F32)).astype(BF16).astype(F32)
        bins_sum = (grad + grad_mirror).astype(BF16)
        back = jnp.dot(weight_t, bins_sum, preferred_element_type=F32)
        for n in range(2):
            o = j + half * n
            dm[HALO + o] = (back[:, tq * n : tq * (n + 1)] * slope2[o]).astype(BF16)
        return carry

    lax.fori_loop(0, half, head, 0)

    finish_d = edges(dm, dh, 1, 8)

    def second_back(o, total):
        ok = row_ok(o - D1)
        for n, (src, dst) in enumerate(((dm, em), (dh, eh))):
            grad = src[o + D2].astype(F32) + total[:, tq * n : tq * (n + 1)]
            delta = grad * slope1[o + D1, :, tq * n : tq * (n + 1)] * ok
            dst[o] = (delta * side_ok if n else delta).astype(BF16)

    conv(w2t, wide_rows(dm, dh, D2), ext, D2, second_back)

    def first_back(m, total):
        for n in range(2):
            o = 2 * m + n
            out[o] = em[o + D1].astype(F32) + total[:, tq * n : tq * (n + 1)]

    conv(w1t, row_pairs(em, eh, D1), (tp + 2 * D1) // 2, D1 // 2, first_back)

    tgt_leave()
    finish_x()
    mir_leave()
    finish_d()


def conv_weights(kernel):
    taps, _, outs, ins = kernel.shape
    return jnp.transpose(kernel, (0, 2, 1, 3)).reshape(taps * outs, taps * ins)


def turned_weights(kernel):
    return conv_weights(jnp.transpose(kernel[::-1, ::-1], (0, 1, 3, 2)))


def local_step(
    rows, cols, pair_features, first_kernel, first_bias, second_kernel, second_bias,
    head_weight, head_bias, target,
):
    ch, tp, tq = pair_features.shape
    bins = head_weight.shape[0]
    padded = -(-bins // 8) * 8
    ext = tp + 2 * HALO
    blocks = -(-ext // PER)
    hw = jnp.pad(head_weight, ((0, padded - bins), (0, 0)))
    hb = jnp.pad(head_bias, (0, padded - bins), constant_values=-1e30)
    vmem = pl.BlockSpec(memory_space=pltpu.VMEM)
    plane = lambda n, dtype=BF16: pltpu.VMEM((n, ch, tq), dtype)
    out = pl.pallas_call(
        functools.partial(kernel, rows, cols),
        out_shape=jax.ShapeDtypeStruct((tp, ch, tq), F32),
        in_specs=[pl.BlockSpec(memory_space=pl.ANY)] + [vmem] * 10,
        out_specs=vmem,
        scratch_shapes=[
            plane(blocks * PER), plane(blocks * PER),
            plane(tp + 2 * D2), plane(tp + 2 * D2),
            plane(blocks * PER), plane(blocks * PER),
            plane(tp + 2 * D1), plane(tp + 2 * D1),
            pltpu.VMEM((ext, 2 * ch, 2 * tq), F32),
            pltpu.VMEM((tp + 2 * D2, ch, 2 * tq), F32),
            plane(tp, F32), plane(tp, F32), plane(tp, F32),
            pltpu.VMEM((2, 2, blocks, ch, tq), BF16),
            pltpu.VMEM((2, 2, blocks, ch, tq), BF16),
            pltpu.VMEM((2, tp // 2, ch, tq), BF16),
            pltpu.VMEM((2, tp // 2, ch, tq), BF16),
            pltpu.VMEM((2, tp // 2, tq), F32),
            pltpu.VMEM((2, tp // 2, tq), F32),
            pltpu.VMEM((tp, tq), F32),
            pltpu.SemaphoreType.DMA((20,)),
            pltpu.SemaphoreType.DMA((20,)),
            pltpu.SemaphoreType.DMA((1,)),
        ],
        compiler_params=pltpu.CompilerParams(
            collective_id=0, has_side_effects=True, vmem_limit_bytes=60 * 1024 * 1024
        ),
    )(
        jnp.transpose(pair_features, (1, 0, 2)),
        conv_weights(first_kernel), turned_weights(first_kernel),
        conv_weights(second_kernel), turned_weights(second_kernel),
        first_bias[:, None], second_bias[:, None], hw, hw.T, hb[:, None], target,
    )
    return jnp.transpose(out, (1, 0, 2))


def solution(mesh):
    placed = (P(None, "col", "row"), P(), P(), P(), P(), P(), P(), P("col", "row"))
    return jax.shard_map(
        functools.partial(local_step, mesh.shape["row"], mesh.shape["col"]),
        mesh=mesh, in_specs=placed, out_specs=P(None, "col", "row"), check_vma=False,
    )
```

time: 494 us -> 251 us (0.51)
  the two profiles are of different devices: /device:TPU:30 before, /device:TPU:97 now
where the time goes in v1:
time: 251 us
  Pallas kernels  233 us (93%)
  local copies, waits for them, and re-layouts  17.7 us (7%)
    pallas_call x1, Pallas kernels, local_step(): pl.pallas_call(functools.partial(kernel, rows, cols), out_shape=jax.Shape...  233 us

profile of v1, /device:TPU:97, one launch (start us, length us, event | category | flops | bytes accessed | tf_op | source)
XLA Modules:
  0.0 250.5 jit_solution(822041928781885417)
XLA Ops:
  0.0 0.0 copy-start.1
  0.0 0.0 copy-start.2
  0.0 0.0 copy-start
  0.0 0.8 pad_bitcast_fusion
  0.8 0.8 copy.25
  1.6 0.1 copy.32
  1.7 0.6 pad_bitcast_fusion.1.hwt
  2.3 0.6 pad.8.clone.hw
  2.9 0.7 copy.29.hb
  3.6 1.4 copy.26.b1
  4.9 1.4 copy.27.b2
  6.3 0.9 reverse_bitcast_fusion.1
  7.2 0.2 copy.22
  7.4 0.8 reshape.13.w1t
  8.2 0.9 reverse_bitcast_fusion
  9.1 0.2 copy.24
  9.3 0.8 reshape.15.w2t
  10.1 0.0 copy-done.1
  10.1 0.1 copy.23
  10.2 0.8 reshape.14.w2
  11.0 0.0 copy-done.2
  11.0 0.1 copy.21
  11.2 0.8 reshape.12.w1
  12.0 0.0 copy-done
  12.0 1.6 copy.33
  13.6 232.7 %shard_map.82 = f32[64,64,128]{2,1,0:T(8,128)} custom-call(bf16[64,64,128]{2,1,0:T(8,128)(2,1)} %bitcast.17, bf16[192,192]{1,0:T(8,128)(2,1)} %reshape.12.w1, bf16[192,192]{1,0:T(8,128)(2,1)} %reshape.13.w1t, bf16[192,192]{1,0:T(8,128)(2,1)} %reshape.14.w2, bf16[192,192]{1,0:T(8,128)(2,1)} %reshape.15.w2t, f32[64,1]{1,0:T(8,128)} %copy.26.b1, ...), custom_call_target="tpu_custom_call" | custom-call | tf_op jit(solution)/shard_map/pallas_call | solution.py:389
  246.4 4.1 %copy.30 = f32[64,64,128]{2,1,0:T(8,128)} copy(f32[64,64,128]{2,0,1:T(8,128)} %bitcast.16) | data formatting | bytes 4194304 | tf_op jit(solution)/shard_map/transpose | solution.py:422
Async XLA Ops:
  0.0 10.1 %copy-start.1 = (bf16[3,3,64,64]{3,2,1,0:T(8,128)(2,1)S(1)}, bf16[3,3,64,64]{3,2,1,0:T(8,128)(2,1)}, u32[]{:S(2)}) copy-start(bf16[3,3,64,64]{3,2,1,0:T(8,128)(2,1)} %param.11) | copy-start | bytes 221188
  0.0 11.0 %copy-start.2 = (bf16[3,3,64,64]{3,2,1,0:T(8,128)(2,1)S(1)}, bf16[3,3,64,64]{3,2,1,0:T(8,128)(2,1)}, u32[]{:S(2)}) copy-start(bf16[3,3,64,64]{3,2,1,0:T(8,128)(2,1)} %param.9) | copy-start | bytes 221188
  0.0 12.0 %copy-start = (bf16[64,64,128]{2,1,0:T(8,128)(2,1)S(1)}, bf16[64,64,128]{2,1,0:T(8,128)(2,1)}, u32[]{:S(2)}) copy-start(bf16[64,64,128]{2,1,0:T(8,128)(2,1)} %param.8) | copy-start | bytes 3145732

commit v2 on v1

--- a/solution.py
+++ b/solution.py
@@ -11,14 +11,17 @@
 D2 = 8
 HALO = D1 + D2
 PER = 128 // HALO
+SPREAD = 4
+HEADS = 2
 MESH = pl.DeviceIdType.MESH
 F32, BF16 = jnp.float32, jnp.bfloat16
 
 
 def kernel(
-    rows, cols, x_hbm, w1, w1t, w2, w2t, b1, b2, hw, hwt, hb, target, out,
-    xm, xh, hm, hh, dm, dh, em, eh, ybuf, slope1, slope2, hid, turned,
-    pack_out, pack_in, mir_out, mir_in, tgt_out, tgt_in, tgt_here, send, recv, local,
+    rows, cols, x_hbm, k1, k2, b1, b2, hw, hb, target, out,
+    xm, xh, hm, hh, dm, dh, em, eh, w1, w1t, w2, w2t, slope1, slope2, hid, turned,
+    pack_out, pack_in, mir_out, mir_in, relay, tgt_out, tgt_in, tgt_here, send, recv, local,
+    leave_sem, enter_sem, pass_sem, land_sem, head_pad, bias_pad, *ybufs,
 ):
     r, c = lax.axis_index("row"), lax.axis_index("col")
     tp, ch, tq = out.shape
@@ -29,8 +32,20 @@
     at_up, at_down = (r, jnp.maximum(c - 1, 0)), (r, jnp.minimum(c + 1, cols - 1))
     at_left, at_right = (jnp.maximum(r - 1, 0), c), (jnp.minimum(r + 1, rows - 1), c)
     partners = [(c // 2, 2 * r), (c // 2, 2 * r + 1)]
-    other = [jnp.logical_or(pr != r, pc != c) for pr, pc in partners]
     mine = c % 2
+    group = rows // SPREAD
+
+    def elsewhere(who):
+        return jnp.logical_or(who[0] != r, who[1] != c)
+
+    other = [elsewhere(who) for who in partners]
+
+    def shifted(row, d):
+        return (row // group + d) % SPREAD * group + row % group
+
+    via = [(shifted(r, d), c) for d in range(SPREAD)]
+    relayed = [[(c // 2, 2 * shifted(r, SPREAD - d) + h) for h in range(2)] for d in range(SPREAD)]
+    relays = [[(shifted(c // 2, d), 2 * r + g) for g in range(2)] for d in range(SPREAD)]
 
     load = pltpu.make_async_copy(x_hbm, xm.at[pl.ds(HALO, tp)], local.at[0])
     load.start()
@@ -38,12 +53,14 @@
     barrier = pltpu.get_barrier_semaphore()
     friends = [(up, at_up), (down, at_down), (left, at_left), (right, at_right)]
     friends += list(zip(other, partners))
-    for there, who in friends:
+    greeted = friends + [(elsewhere(who), who) for d in range(1, SPREAD) for who in relays[d]]
+    friends = friends + [(elsewhere(who), who) for d in range(1, SPREAD) for who in relayed[d]]
+    for d in range(1, SPREAD):
+        pl.semaphore_signal(barrier, inc=1, device_id=via[d], device_id_type=MESH)
+    for there, who in greeted:
         @pl.when(there)
         def _(who=who):
             pl.semaphore_signal(barrier, inc=1, device_id=who, device_id_type=MESH)
-    pl.semaphore_wait(barrier, sum(there.astype(jnp.int32) for there, _ in friends))
-
     lane = lax.broadcasted_iota(jnp.int32, (ch, tq), 1)
     low = lane < tq // 2
 
@@ -61,6 +78,15 @@
         a = whole[tp * h : tp * h + half]
         b = whole[tp * h + half : tp * (h + 1)]
         tgt_out[h] = jnp.where(low_rows, a, b)
+    for kernel_ref, straight, turned_ref in ((k1, w1, w1t), (k2, w2, w2t)):
+        for t in range(3):
+            blocks_t = [kernel_ref[t, n] for n in range(3)]
+            straight[pl.ds(ch * t, ch)] = jnp.concatenate(blocks_t, axis=1)
+            back = [jnp.transpose(kernel_ref[2 - t, 2 - n].astype(F32)) for n in range(3)]
+            turned_ref[pl.ds(ch * t, ch)] = jnp.concatenate(back, axis=1).astype(BF16)
+    bias1 = jnp.transpose(jnp.broadcast_to(b1[...], (tq, ch)))
+    bias2 = jnp.transpose(jnp.broadcast_to(b2[...], (tq, ch)))
+
     def swap(src, dst, k):
         outgoing = [
             remote(src.at[h], dst.at[mine], k + h, partners[h], k + mine) for h in range(2)
@@ -89,9 +115,7 @@
 
         return arrive, leave
 
-    tgt_arrive, tgt_leave = swap(tgt_out, tgt_in, 16)
-
-    def edges(main, halo, which, base):
+    def edges(main, halo, which, base, ready):
         first = remote(main.at[pl.ds(HALO, HALO)], main.at[pl.ds(HALO + tp, HALO)], base, at_up)
         last = remote(main.at[pl.ds(tp, HALO)], main.at[pl.ds(0, HALO)], base + 1, at_down)
         parts = [(2, blocks - 4), (0, 2), (blocks - 2, 2)]
@@ -104,27 +128,19 @@
                 base + 2 + 3 * s + n, (at_left, at_right)[s],
             )
 
-        @pl.when(up)
-        def _():
-            first.start()
-
-        @pl.when(down)
-        def _():
-            last.start()
-
         def pack(b, carry):
-            first_lanes = jnp.zeros((ch, tq), F32)
-            last_lanes = jnp.zeros((ch, tq), F32)
+            first_lanes = jnp.zeros((ch, tq), BF16)
+            last_lanes = jnp.zeros((ch, tq), BF16)
             for j in range(PER):
-                row = main[b * PER + j].astype(F32)
+                row = main[b * PER + j]
                 slot = jnp.logical_and(lane >= HALO * j, lane < HALO * (j + 1))
-                shifted = pltpu.roll(row, HALO * j, 1) if j else row
-                first_lanes = jnp.where(slot, shifted, first_lanes)
+                moved = pltpu.roll(row, HALO * j, 1) if j else row
+                first_lanes = jnp.where(slot, moved, first_lanes)
                 last_lanes = jnp.where(
-                    slot, pltpu.roll(row, (HALO * (j + 1)) % tq, 1), last_lanes
+                    slot, pltpu.roll(row, HALO * (j + 1), 1), last_lanes
                 )
-            pack_out[which, 0, b] = first_lanes.astype(BF16)
-            pack_out[which, 1, b] = last_lanes.astype(BF16)
+            pack_out[which, 0, b] = first_lanes
+            pack_out[which, 1, b] = last_lanes
             return carry
 
         def begin(n):
@@ -137,6 +153,16 @@
                 side(1, n).start()
 
         lax.fori_loop(2, blocks - 2, pack, 0)
+        ready()
+
+        @pl.when(up)
+        def _():
+            first.start()
+
+        @pl.when(down)
+        def _():
+            last.start()
+
         begin(0)
 
         @pl.when(down)
@@ -175,12 +201,12 @@
                 pack_in[which, s] = jnp.zeros(pack_in.shape[2:], BF16)
 
         def unpack(b, carry):
-            after = pack_in[which, 0, b].astype(F32)
-            before = pack_in[which, 1, b].astype(F32)
+            after = pack_in[which, 0, b]
+            before = pack_in[which, 1, b]
             for j in range(PER):
                 a = pltpu.roll(after, (-HALO * j) % tq, 1) if j else after
                 z = pltpu.roll(before, (-HALO * (j + 1)) % tq, 1)
-                halo[b * PER + j] = jnp.where(low, a, z).astype(BF16)
+                halo[b * PER + j] = jnp.where(low, a, z)
             return carry
 
         lax.fori_loop(0, blocks, unpack, 0)
@@ -210,39 +236,52 @@
         rm, rh = pltpu.roll(main, d, 1), pltpu.roll(halo, d, 1)
         head, tail = lane < d, lane >= tq - d
         first = [jnp.where(head, rh, rm), main, jnp.where(tail, lh, lm)]
-        first = jnp.concatenate(first, axis=0).astype(BF16)
+        first = jnp.concatenate(first, axis=0)
         if not wide:
             return first
         second = [jnp.where(head, rm, rh), halo, jnp.where(tail, lm, lh)]
-        return jnp.concatenate([first, jnp.concatenate(second, axis=0).astype(BF16)], axis=1)
+        return jnp.concatenate([first, jnp.concatenate(second, axis=0)], axis=1)
 
     def conv(weights, patches, count, lag, done):
         w = weights[...]
 
-        def step(j, finish):
-            y = jnp.dot(w, patches(j), preferred_element_type=F32)
-            ybuf[j] = y[: 2 * ch]
-            if finish:
-                done(j - 2 * lag, ybuf[j - 2 * lag, :ch] + ybuf[j - lag, ch:] + y[2 * ch :])
-
-        def loop(lo, hi, finish):
-            def body(j, carry):
-                step(lo + 2 * j, finish)
-                step(lo + 2 * j + 1, finish)
-                return carry
-
-            lax.fori_loop(0, (hi - lo) // 2, body, 0)
-
-        loop(0, 2 * lag, False)
-        loop(2 * lag, count, True)
+        unroll = 4
+
+        def body(b, finish):
+            ys = []
+            for n in range(unroll):
+                def older(back, part):
+                    k = n - back * lag
+                    span = pl.ds(ch * part, ch)
+                    if k >= 0:
+                        return ys[k][ch * part : ch * (part + 1)]
+                    return ybufs[k % unroll][b + k // unroll, span]
+
+                j = b * unroll + n
+                before = older(2, 0) + older(1, 1) if finish else None
+                y = jnp.dot(w, patches(j), preferred_element_type=F32)
+                ys.append(y)
+                if finish:
+                    done(j - 2 * lag, before + y[2 * ch :])
+                ybufs[n][b] = y[: 2 * ch]
+
+        start = 2 * lag // unroll
+        for b in range(start):
+            body(b, False)
+
+        def again(b, carry):
+            body(b, True)
+            return carry
+
+        lax.fori_loop(start, count // unroll, again, 0)
 
     def wide_rows(main, halo, d):
-        return lambda j: taps(main[j].astype(F32), halo[j].astype(F32), d, True)
+        return lambda j: taps(main[j], halo[j], d, True)
 
     def row_pairs(main, halo, d):
         def patches(j):
-            one = taps(main[2 * j].astype(F32), halo[2 * j].astype(F32), d, False)
-            two = taps(main[2 * j + 1].astype(F32), halo[2 * j + 1].astype(F32), d, False)
+            one = taps(main[2 * j], halo[2 * j], d, False)
+            two = taps(main[2 * j + 1], halo[2 * j + 1], d, False)
             return jnp.concatenate([one, two], axis=1)
 
         return patches
@@ -258,9 +297,16 @@
     if pad:
         xm[pl.ds(ext, pad)] = jnp.zeros((pad, ch, tq), BF16)
         dm[pl.ds(ext, pad)] = jnp.zeros((pad, ch, tq), BF16)
-    finish_x = edges(xm, xh, 0, 0)
-    bias1 = jnp.broadcast_to(b1[...], (ch, tq))
-    bias2 = jnp.broadcast_to(b2[...], (ch, tq))
+    tgt_swap = []
+
+    def enter():
+        pl.semaphore_wait(
+            barrier, SPREAD - 1 + sum(there.astype(jnp.int32) for there, _ in friends)
+        )
+        tgt_swap.extend(swap(tgt_out, tgt_in, 16))
+
+    finish_x = edges(xm, xh, 0, 0, enter)
+    tgt_arrive, tgt_leave = tgt_swap
 
     def first_done(o, total):
         ok = row_ok(o - D2)
@@ -283,31 +329,111 @@
 
     conv(w2, row_pairs(hm, hh, D2), (tp + 2 * D2) // 2, D2 // 2, second_done)
 
-    def turn(o, carry):
-        plane = hid[:, o, :]
-        plane = jnp.transpose(jnp.concatenate([plane, plane], axis=0))
+    def turn(n, carry):
+        for k in range(4):
+            o = 4 * n + k
+            plane = hid[:, o, :]
+            plane = jnp.transpose(jnp.concatenate([plane, plane], axis=0))
+            for h in range(2):
+                a = plane[tp * h : tp * h + half]
+                b = plane[tp * h + half : tp * (h + 1)]
+                turned[pl.ds(half * h, half), o, :] = jnp.where(low_rows, a, b)
+        return carry
+
+    lax.fori_loop(0, ch // 4, turn, 0)
+
+    chunk = half // SPREAD
+    spans = [pl.ds(chunk * d, chunk) for d in range(SPREAD)]
+
+    def first_leg(h, d):
+        if d == 0:
+            return pltpu.make_async_remote_copy(
+                src_ref=mir_out.at[h, spans[0]], dst_ref=mir_in.at[mine, spans[0]],
+                send_sem=leave_sem.at[h, 0], recv_sem=land_sem.at[mine, 0],
+                device_id=partners[h], device_id_type=MESH,
+            )
+        return pltpu.make_async_remote_copy(
+            src_ref=mir_out.at[h, spans[d]], dst_ref=relay.at[d - 1, h],
+            send_sem=leave_sem.at[h, d], recv_sem=enter_sem.at[h, d],
+            device_id=via[d], device_id_type=MESH,
+        )
+
+    def last_leg(h, d):
+        return pltpu.make_async_remote_copy(
+            src_ref=relay.at[d - 1, h], dst_ref=mir_in.at[mine, spans[d]],
+            send_sem=pass_sem.at[h, d], recv_sem=land_sem.at[mine, d],
+            device_id=relayed[d][h], device_id_type=MESH,
+        )
+
+    def landing(g, d):
+        return pltpu.make_async_remote_copy(
+            src_ref=mir_out.at[g, spans[d]], dst_ref=mir_in.at[g, spans[d]],
+            send_sem=leave_sem.at[g, d], recv_sem=land_sem.at[g, d],
+            device_id=relays[d][g], device_id_type=MESH,
+        )
+
+    order = [d for d in (1, 3, 2, 0) if d < SPREAD]
+    for d in order:
+        def settle(j, carry, d=d):
+            for h in range(2):
+                mir_out[h, chunk * d + j] = turned[half * h + chunk * d + j].astype(BF16)
+            return carry
+
+        lax.fori_loop(0, chunk, settle, 0)
         for h in range(2):
-            a = plane[tp * h : tp * h + half]
-            b = plane[tp * h + half : tp * (h + 1)]
-            turned[pl.ds(half * h, half), o, :] = jnp.where(low_rows, a, b)
-        return carry
-
-    lax.fori_loop(0, ch, turn, 0)
-
-    def settle(j, carry):
-        mir_out[0, j] = turned[j].astype(BF16)
-        mir_out[1, j] = turned[half + j].astype(BF16)
-        return carry
-
-    lax.fori_loop(0, half, settle, 0)
-
-    mir_arrive, mir_leave = swap(mir_out, mir_in, 18)
+            if d:
+                first_leg(h, d).start()
+            else:
+                @pl.when(other[h])
+                def _(h=h):
+                    first_leg(h, 0).start()
+
+                @pl.when(jnp.logical_not(other[h]))
+                def _(h=h):
+                    mir_in[h, spans[0]] = mir_out[h, spans[0]]
+
+    for d in order[:-1]:
+        for h in range(2):
+            first_leg(h, d).wait_recv()
+
+            @pl.when(elsewhere(relayed[d][h]))
+            def _(h=h, d=d):
+                last_leg(h, d).start()
+
+            @pl.when(jnp.logical_not(elsewhere(relayed[d][h])))
+            def _(h=h, d=d):
+                mir_in[mine, spans[d]] = relay[d - 1, h]
+
+    def mir_arrive(d):
+        for g in range(2):
+            @pl.when(elsewhere(relays[d][g]))
+            def _(g=g):
+                landing(g, d).wait_recv()
+
+    def mir_leave():
+        for h in range(2):
+            @pl.when(other[h])
+            def _(h=h):
+                first_leg(h, 0).wait_send()
+
+            for d in range(1, SPREAD):
+                first_leg(h, d).wait_send()
+
+                @pl.when(elsewhere(relayed[d][h]))
+                def _(h=h, d=d):
+                    last_leg(h, d).wait_send()
+
     tgt_arrive()
-    mir_arrive()
-
-    weight, weight_t = hw[...], hwt[...]
-    bins = weight.shape[0]
-    bias = jnp.broadcast_to(hb[...], (bins, 2 * tq))
+
+    real = hw.shape[0]
+    bins = bias_pad.shape[0]
+    head_pad[...] = jnp.zeros_like(head_pad)
+    head_pad[pl.ds(0, real), pl.ds(0, ch)] = hw[...].astype(F32)
+    weight = head_pad[...][:bins, :ch].astype(BF16)
+    weight_t = jnp.transpose(head_pad[...])[:ch, :bins].astype(BF16)
+    bias_pad[...] = jnp.full_like(bias_pad, -1e30)
+    bias_pad[pl.ds(0, real)] = jnp.transpose(jnp.broadcast_to(hb[...], (tq, real)))
+    bias = jnp.concatenate([bias_pad[...], bias_pad[...]], axis=1)
     bin_ids = lax.broadcasted_iota(jnp.int32, (bins, 2 * tq), 0).astype(F32)
     low_row = lax.broadcasted_iota(jnp.int32, (1, tq), 1) < tq // 2
 
@@ -318,7 +444,7 @@
 
     tgt_here[...] = target[...].astype(F32)
 
-    def head(j, carry):
+    def head(j):
         mirrored = facing(mir_in[0, j].astype(F32), mir_in[1, j].astype(F32), low)
         own = jnp.concatenate([hid[j], hid[j + half]], axis=1)
         symmetric = (own + mirrored).astype(BF16)
@@ -336,11 +462,18 @@
         for n in range(2):
             o = j + half * n
             dm[HALO + o] = (back[:, tq * n : tq * (n + 1)] * slope2[o]).astype(BF16)
-        return carry
-
-    lax.fori_loop(0, half, head, 0)
-
-    finish_d = edges(dm, dh, 1, 8)
+
+    for d in (order[-1:] + order[:-1]):
+        mir_arrive(d)
+
+        def heads(n, carry, d=d):
+            for k in range(HEADS):
+                head(chunk * d + HEADS * n + k)
+            return carry
+
+        lax.fori_loop(0, chunk // HEADS, heads, 0)
+
+    finish_d = edges(dm, dh, 1, 8, lambda: None)
 
     def second_back(o, total):
         ok = row_ok(o - D1)
@@ -364,60 +497,51 @@
     finish_d()
 
 
-def conv_weights(kernel):
-    taps, _, outs, ins = kernel.shape
-    return jnp.transpose(kernel, (0, 2, 1, 3)).reshape(taps * outs, taps * ins)
-
-
-def turned_weights(kernel):
-    return conv_weights(jnp.transpose(kernel[::-1, ::-1], (0, 1, 3, 2)))
-
-
 def local_step(
     rows, cols, pair_features, first_kernel, first_bias, second_kernel, second_bias,
     head_weight, head_bias, target,
 ):
     ch, tp, tq = pair_features.shape
-    bins = head_weight.shape[0]
-    padded = -(-bins // 8) * 8
     ext = tp + 2 * HALO
     blocks = -(-ext // PER)
-    hw = jnp.pad(head_weight, ((0, padded - bins), (0, 0)))
-    hb = jnp.pad(head_bias, (0, padded - bins), constant_values=-1e30)
     vmem = pl.BlockSpec(memory_space=pltpu.VMEM)
     plane = lambda n, dtype=BF16: pltpu.VMEM((n, ch, tq), dtype)
     out = pl.pallas_call(
         functools.partial(kernel, rows, cols),
         out_shape=jax.ShapeDtypeStruct((tp, ch, tq), F32),
-        in_specs=[pl.BlockSpec(memory_space=pl.ANY)] + [vmem] * 10,
+        in_specs=[pl.BlockSpec(memory_space=pl.ANY)] + [vmem] * 7,
         out_specs=vmem,
         scratch_shapes=[
             plane(blocks * PER), plane(blocks * PER),
             plane(tp + 2 * D2), plane(tp + 2 * D2),
             plane(blocks * PER), plane(blocks * PER),
             plane(tp + 2 * D1), plane(tp + 2 * D1),
-            pltpu.VMEM((ext, 2 * ch, 2 * tq), F32),
+            *[pltpu.VMEM((3 * ch, 3 * ch), BF16)] * 4,
             pltpu.VMEM((tp + 2 * D2, ch, 2 * tq), F32),
             plane(tp, F32), plane(tp, F32), plane(tp, F32),
             pltpu.VMEM((2, 2, blocks, ch, tq), BF16),
             pltpu.VMEM((2, 2, blocks, ch, tq), BF16),
             pltpu.VMEM((2, tp // 2, ch, tq), BF16),
             pltpu.VMEM((2, tp // 2, ch, tq), BF16),
+            pltpu.VMEM((SPREAD - 1, 2, tp // 2 // SPREAD, ch, tq), BF16),
             pltpu.VMEM((2, tp // 2, tq), F32),
             pltpu.VMEM((2, tp // 2, tq), F32),
             pltpu.VMEM((tp, tq), F32),
-            pltpu.SemaphoreType.DMA((20,)),
-            pltpu.SemaphoreType.DMA((20,)),
+            pltpu.SemaphoreType.DMA((18,)),
+            pltpu.SemaphoreType.DMA((18,)),
             pltpu.SemaphoreType.DMA((1,)),
+            *[pltpu.SemaphoreType.DMA((2, SPREAD))] * 4,
+            pltpu.VMEM((128, 128), F32),
+            pltpu.VMEM((-(-head_weight.shape[0] // 8) * 8, tq), F32),
+            *[pltpu.VMEM((ext // 4 , 2 * ch, 2 * tq), F32) for n in range(8)],
         ],
         compiler_params=pltpu.CompilerParams(
             collective_id=0, has_side_effects=True, vmem_limit_bytes=60 * 1024 * 1024
         ),
     )(
         jnp.transpose(pair_features, (1, 0, 2)),
-        conv_weights(first_kernel), turned_weights(first_kernel),
-        conv_weights(second_kernel), turned_weights(second_kernel),
-        first_bias[:, None], second_bias[:, None], hw, hw.T, hb[:, None], target,
+        first_kernel, second_kernel, first_bias[None], second_bias[None],
+        head_weight, head_bias[None], target,
     )
     return jnp.transpose(out, (1, 0, 2))
 

time: 251 us -> 167 us (0.67)
  the two profiles are of different devices: /device:TPU:97 before, /device:TPU:57 now
where the time goes in v2:
time: 167 us
  Pallas kernels  160 us (96%)
  local copies, waits for them, and re-layouts  7 us (4%)
    pallas_call x1, Pallas kernels, local_step(): pl.pallas_call(functools.partial(kernel, rows, cols), out_shape=jax.Shape...  160 us
    transpose x1, local copies, waits for them, and re-layouts, local_step(): return jnp.transpose(out, (1, 0, 2))  4.13 us

profile of v2, /device:TPU:57, one launch (start us, length us, event | category | flops | bytes accessed | tf_op | source)
XLA Modules:
  0.0 166.5 jit_solution(11349181159718552289)
XLA Ops:
  0.0 2.9 %copy.12 = bf16[64,64,128]{2,0,1:T(8,128)(2,1)} copy(bf16[64,64,128]{2,1,0:T(8,128)(2,1)} %param.8) | data formatting | bytes 2097152 | tf_op args[0]
  2.9 159.5 %shard_map.82 = f32[64,64,128]{2,1,0:T(8,128)} custom-call(bf16[64,64,128]{2,1,0:T(8,128)(2,1)} %bitcast.8, bf16[3,3,64,64]{3,2,1,0:T(8,128)(2,1)} %k1.1, bf16[3,3,64,64]{3,2,1,0:T(8,128)(2,1)} %k2.1, f32[1,64]{1,0:T(1,128)} %bitcast.9, f32[1,64]{1,0:T(1,128)} %bitcast.10, bf16[37,64]{1,0:T(8,128)(2,1)} %hw.1, f32[1,37]{1,0:T(1,128)} %bitcast.11, ...), custom_call_target="tpu_custom_call" | custom-call | tf_op jit(solution)/shard_map/pallas_call | solution.py:509
  162.4 4.1 %copy.10 = f32[64,64,128]{2,1,0:T(8,128)} copy(f32[64,64,128]{2,0,1:T(8,128)} %bitcast.7) | data formatting | bytes 4194304 | tf_op jit(solution)/shard_map/transpose | solution.py:546

commit v3 on v2

--- a/solution.py
+++ b/solution.py
@@ -12,6 +12,7 @@
 HALO = D1 + D2
 PER = 128 // HALO
 SPREAD = 4
+SETS = 2
 HEADS = 2
 MESH = pl.DeviceIdType.MESH
 F32, BF16 = jnp.float32, jnp.bfloat16
@@ -21,10 +22,10 @@
     rows, cols, x_hbm, k1, k2, b1, b2, hw, hb, target, out,
     xm, xh, hm, hh, dm, dh, em, eh, w1, w1t, w2, w2t, slope1, slope2, hid, turned,
     pack_out, pack_in, mir_out, mir_in, relay, tgt_out, tgt_in, tgt_here, send, recv, local,
-    leave_sem, enter_sem, pass_sem, land_sem, head_pad, bias_pad, *ybufs,
+    leave_sem, enter_sem, pass_sem, land_sem, x_in, head_pad, bias_pad, *ybufs,
 ):
     r, c = lax.axis_index("row"), lax.axis_index("col")
-    tp, ch, tq = out.shape
+    ch, tp, tq = out.shape
     half = tp // 2
     ext = tp + 2 * HALO
     blocks = pack_in.shape[2]
@@ -47,7 +48,7 @@
     relayed = [[(c // 2, 2 * shifted(r, SPREAD - d) + h) for h in range(2)] for d in range(SPREAD)]
     relays = [[(shifted(c // 2, d), 2 * r + g) for g in range(2)] for d in range(SPREAD)]
 
-    load = pltpu.make_async_copy(x_hbm, xm.at[pl.ds(HALO, tp)], local.at[0])
+    load = pltpu.make_async_copy(x_hbm, x_in, local.at[0])
     load.start()
 
     barrier = pltpu.get_barrier_semaphore()
@@ -71,12 +72,18 @@
             device_id=who, device_id_type=MESH,
         )
 
+    part = half // SETS
+
+    def outer_first(rows_of_half):
+        pieces = [rows_of_half[part * n : part * (n + 1)] for n in range(SETS)]
+        return jnp.concatenate(pieces[::-1], axis=0)
+
     whole = target[...].astype(F32)
     whole = jnp.transpose(jnp.concatenate([whole, whole], axis=0))
     low_rows = lax.broadcasted_iota(jnp.int32, (half, tq), 1) < tq // 2
     for h in range(2):
         a = whole[tp * h : tp * h + half]
-        b = whole[tp * h + half : tp * (h + 1)]
+        b = outer_first(whole[tp * h + half : tp * (h + 1)])
         tgt_out[h] = jnp.where(low_rows, a, b)
     for kernel_ref, straight, turned_ref in ((k1, w1, w1t), (k2, w2, w2t)):
         for t in range(3):
@@ -115,10 +122,9 @@
 
         return arrive, leave
 
-    def edges(main, halo, which, base, ready):
+    def edges(main, halo, which, base, parts):
         first = remote(main.at[pl.ds(HALO, HALO)], main.at[pl.ds(HALO + tp, HALO)], base, at_up)
         last = remote(main.at[pl.ds(tp, HALO)], main.at[pl.ds(0, HALO)], base + 1, at_down)
-        parts = [(2, blocks - 4), (0, 2), (blocks - 2, 2)]
 
         def side(s, n):
             lo, count = parts[n]
@@ -127,6 +133,15 @@
                 pack_out.at[which, s, span], pack_in.at[which, s, span],
                 base + 2 + 3 * s + n, (at_left, at_right)[s],
             )
+
+        def send_rows():
+            @pl.when(up)
+            def _():
+                first.start()
+
+            @pl.when(down)
+            def _():
+                last.start()
 
         def pack(b, carry):
             first_lanes = jnp.zeros((ch, tq), BF16)
@@ -136,13 +151,14 @@
                 slot = jnp.logical_and(lane >= HALO * j, lane < HALO * (j + 1))
                 moved = pltpu.roll(row, HALO * j, 1) if j else row
                 first_lanes = jnp.where(slot, moved, first_lanes)
-                last_lanes = jnp.where(
-                    slot, pltpu.roll(row, HALO * (j + 1), 1), last_lanes
-                )
+                last_lanes = jnp.where(slot, pltpu.roll(row, HALO * (j + 1), 1), last_lanes)
             pack_out[which, 0, b] = first_lanes
             pack_out[which, 1, b] = last_lanes
             return carry
 
+        def fill(n):
+            lax.fori_loop(parts[n][0], sum(parts[n]), pack, 0)
+
         def begin(n):
             @pl.when(left)
             def _():
@@ -152,53 +168,22 @@
             def _():
                 side(1, n).start()
 
-        lax.fori_loop(2, blocks - 2, pack, 0)
-        ready()
-
-        @pl.when(up)
-        def _():
-            first.start()
-
-        @pl.when(down)
-        def _():
-            last.start()
-
-        begin(0)
-
-        @pl.when(down)
-        def _():
-            first.wait_recv()
-
-        @pl.when(jnp.logical_not(down))
-        def _():
-            main[pl.ds(HALO + tp, HALO)] = jnp.zeros((HALO, ch, tq), BF16)
-
-        @pl.when(up)
-        def _():
-            last.wait_recv()
-
-        @pl.when(jnp.logical_not(up))
-        def _():
-            main[pl.ds(0, HALO)] = jnp.zeros((HALO, ch, tq), BF16)
-
-        lax.fori_loop(0, 2, pack, 0)
-        begin(1)
-        lax.fori_loop(blocks - 2, blocks, pack, 0)
-        begin(2)
-
-        for n in range(3):
-            @pl.when(right)
-            def _(n=n):
-                side(0, n).wait_recv()
-
-            @pl.when(left)
-            def _(n=n):
-                side(1, n).wait_recv()
-
-        for s, there in ((0, right), (1, left)):
-            @pl.when(jnp.logical_not(there))
-            def _(s=s):
-                pack_in[which, s] = jnp.zeros(pack_in.shape[2:], BF16)
+        def take_rows():
+            @pl.when(down)
+            def _():
+                first.wait_recv()
+
+            @pl.when(jnp.logical_not(down))
+            def _():
+                main[pl.ds(HALO + tp, HALO)] = jnp.zeros((HALO, ch, tq), BF16)
+
+            @pl.when(up)
+            def _():
+                last.wait_recv()
+
+            @pl.when(jnp.logical_not(up))
+            def _():
+                main[pl.ds(0, HALO)] = jnp.zeros((HALO, ch, tq), BF16)
 
         def unpack(b, carry):
             after = pack_in[which, 0, b]
@@ -209,7 +194,18 @@
                 halo[b * PER + j] = jnp.where(low, a, z)
             return carry
 
-        lax.fori_loop(0, blocks, unpack, 0)
+        def take(n):
+            lo, count = parts[n]
+            for s, there in ((0, right), (1, left)):
+                @pl.when(there)
+                def _(s=s):
+                    side(s, n).wait_recv()
+
+                @pl.when(jnp.logical_not(there))
+                def _(s=s):
+                    pack_in[which, s, pl.ds(lo, count)] = jnp.zeros((count, ch, tq), BF16)
+
+            lax.fori_loop(lo, lo + count, unpack, 0)
 
         def finish():
             @pl.when(up)
@@ -229,7 +225,7 @@
                 def _(n=n):
                     side(1, n).wait_send()
 
-        return finish
+        return send_rows, fill, begin, take_rows, take, finish
 
     def taps(main, halo, d, wide):
         lm, lh = pltpu.roll(main, tq - d, 1), pltpu.roll(halo, tq - d, 1)
@@ -242,7 +238,7 @@
         second = [jnp.where(head, rm, rh), halo, jnp.where(tail, lm, lh)]
         return jnp.concatenate([first, jnp.concatenate(second, axis=0)], axis=1)
 
-    def conv(weights, patches, count, lag, done):
+    def conv(weights, patches, lag, done, *ranges):
         w = weights[...]
 
         unroll = 4
@@ -265,15 +261,16 @@
                     done(j - 2 * lag, before + y[2 * ch :])
                 ybufs[n][b] = y[: 2 * ch]
 
-        start = 2 * lag // unroll
-        for b in range(start):
-            body(b, False)
-
         def again(b, carry):
             body(b, True)
             return carry
 
-        lax.fori_loop(start, count // unroll, again, 0)
+        start = 2 * lag // unroll
+        for before_span, lo, hi in ranges:
+            before_span()
+            for b in range(lo // unroll, lo // unroll + start):
+                body(b, False)
+            lax.fori_loop(lo // unroll + start, hi // unroll, again, 0)
 
     def wide_rows(main, halo, d):
         return lambda j: taps(main[j], halo[j], d, True)
@@ -293,20 +290,44 @@
         return jnp.where(inside, 1.0, 0.0).astype(F32)
 
     load.wait()
+
+    def spread(n, carry):
+        for k in range(4):
+            hid[:, 4 * n + k, :] = x_in[4 * n + k].astype(F32)
+        return carry
+
+    def gather(n, carry):
+        for k in range(4):
+            xm[HALO + 4 * n + k] = hid[4 * n + k].astype(BF16)
+        return carry
+
+    lax.fori_loop(0, ch // 4, spread, 0)
+    lax.fori_loop(0, tp // 4, gather, 0)
     pad = blocks * PER - ext
     if pad:
         xm[pl.ds(ext, pad)] = jnp.zeros((pad, ch, tq), BF16)
         dm[pl.ds(ext, pad)] = jnp.zeros((pad, ch, tq), BF16)
-    tgt_swap = []
-
-    def enter():
-        pl.semaphore_wait(
-            barrier, SPREAD - 1 + sum(there.astype(jnp.int32) for there, _ in friends)
-        )
-        tgt_swap.extend(swap(tgt_out, tgt_in, 16))
-
-    finish_x = edges(xm, xh, 0, 0, enter)
-    tgt_arrive, tgt_leave = tgt_swap
+    send_rows, fill, begin, take_rows, take, finish_x = edges(
+        xm, xh, 0, 0, [(2, blocks - 4), (0, 2), (blocks - 2, 2)]
+    )
+    fill(0)
+    pl.semaphore_wait(
+        barrier, SPREAD - 1 + sum(there.astype(jnp.int32) for there, _ in friends)
+    )
+    send_rows()
+    begin(0)
+    tgt_arrive, tgt_leave = swap(tgt_out, tgt_in, 16)
+    take_rows()
+    for n in (1, 2):
+        fill(n)
+        begin(n)
+
+    def corners():
+        take(1)
+        take(2)
+
+    nothing = lambda: None
+    inner, outer = 2 * PER, (blocks - 2) * PER // 4 * 4
 
     def first_done(o, total):
         ok = row_ok(o - D2)
@@ -317,7 +338,11 @@
             act = jnp.where(pre > 0, pre, e - 1.0) * ok
             dst[o] = (act * side_ok if n else act).astype(BF16)
 
-    conv(w1, wide_rows(xm, xh, D1), ext, D1, first_done)
+    conv(
+        w1, wide_rows(xm, xh, D1), D1, first_done,
+        (lambda: take(0), inner, outer), (corners, 0, inner + 2 * D1),
+        (nothing, outer - 2 * D1, ext),
+    )
 
     def second_done(m, total):
         for n in range(2):
@@ -327,7 +352,7 @@
             slope2[o] = jnp.where(pre > 0, 1.0, e)
             hid[o] = jnp.where(pre > 0, pre, e - 1.0).astype(BF16).astype(F32)
 
-    conv(w2, row_pairs(hm, hh, D2), (tp + 2 * D2) // 2, D2 // 2, second_done)
+    conv(w2, row_pairs(hm, hh, D2), D2 // 2, second_done, (nothing, 0, (tp + 2 * D2) // 2))
 
     def turn(n, carry):
         for k in range(4):
@@ -336,92 +361,111 @@
             plane = jnp.transpose(jnp.concatenate([plane, plane], axis=0))
             for h in range(2):
                 a = plane[tp * h : tp * h + half]
-                b = plane[tp * h + half : tp * (h + 1)]
+                b = outer_first(plane[tp * h + half : tp * (h + 1)])
                 turned[pl.ds(half * h, half), o, :] = jnp.where(low_rows, a, b)
         return carry
 
     lax.fori_loop(0, ch // 4, turn, 0)
 
-    chunk = half // SPREAD
-    spans = [pl.ds(chunk * d, chunk) for d in range(SPREAD)]
-
-    def first_leg(h, d):
-        if d == 0:
-            return pltpu.make_async_remote_copy(
-                src_ref=mir_out.at[h, spans[0]], dst_ref=mir_in.at[mine, spans[0]],
-                send_sem=leave_sem.at[h, 0], recv_sem=land_sem.at[mine, 0],
-                device_id=partners[h], device_id_type=MESH,
-            )
+    chunk = part // SPREAD
+
+    def span(s, d):
+        return pl.ds(part * s + chunk * d, chunk)
+
+    def travel(src, dst, leaves, lands, who):
         return pltpu.make_async_remote_copy(
-            src_ref=mir_out.at[h, spans[d]], dst_ref=relay.at[d - 1, h],
-            send_sem=leave_sem.at[h, d], recv_sem=enter_sem.at[h, d],
-            device_id=via[d], device_id_type=MESH,
+            src_ref=src, dst_ref=dst, send_sem=leaves, recv_sem=lands,
+            device_id=who, device_id_type=MESH,
         )
 
-    def last_leg(h, d):
-        return pltpu.make_async_remote_copy(
-            src_ref=relay.at[d - 1, h], dst_ref=mir_in.at[mine, spans[d]],
-            send_sem=pass_sem.at[h, d], recv_sem=land_sem.at[mine, d],
-            device_id=relayed[d][h], device_id_type=MESH,
+    def direct(h, s):
+        return travel(
+            mir_out.at[h, span(s, 0)], mir_in.at[mine, span(s, 0)],
+            leave_sem.at[s, h, 0], land_sem.at[s, mine, 0], partners[h],
         )
 
-    def landing(g, d):
-        return pltpu.make_async_remote_copy(
-            src_ref=mir_out.at[g, spans[d]], dst_ref=mir_in.at[g, spans[d]],
-            send_sem=leave_sem.at[g, d], recv_sem=land_sem.at[g, d],
-            device_id=relays[d][g], device_id_type=MESH,
+    def first_leg(h, s, d):
+        return travel(
+            mir_out.at[h, span(s, d)], relay.at[s, d - 1, h],
+            leave_sem.at[s, h, d], enter_sem.at[s, h, d], via[d],
         )
 
-    order = [d for d in (1, 3, 2, 0) if d < SPREAD]
-    for d in order:
-        def settle(j, carry, d=d):
+    def last_leg(h, s, d):
+        return travel(
+            relay.at[s, d - 1, h], mir_in.at[mine, span(s, d)],
+            pass_sem.at[s, h, d], land_sem.at[s, mine, d], relayed[d][h],
+        )
+
+    def landing(g, s, d):
+        return travel(
+            mir_out.at[g, span(s, d)], mir_in.at[g, span(s, d)],
+            leave_sem.at[s, g, d], land_sem.at[s, g, d], relays[d][g],
+        )
+
+    def depart(s, d):
+        def settle(j, carry):
             for h in range(2):
-                mir_out[h, chunk * d + j] = turned[half * h + chunk * d + j].astype(BF16)
+                k = part * s + chunk * d + j
+                mir_out[h, k] = turned[half * h + k].astype(BF16)
             return carry
 
         lax.fori_loop(0, chunk, settle, 0)
         for h in range(2):
             if d:
-                first_leg(h, d).start()
+                first_leg(h, s, d).start()
             else:
                 @pl.when(other[h])
                 def _(h=h):
-                    first_leg(h, 0).start()
+                    direct(h, s).start()
 
                 @pl.when(jnp.logical_not(other[h]))
                 def _(h=h):
-                    mir_in[h, spans[0]] = mir_out[h, spans[0]]
-
-    for d in order[:-1]:
+                    mir_in[h, span(s, 0)] = mir_out[h, span(s, 0)]
+
+    def forward(s, d):
         for h in range(2):
-            first_leg(h, d).wait_recv()
+            first_leg(h, s, d).wait_recv()
 
             @pl.when(elsewhere(relayed[d][h]))
-            def _(h=h, d=d):
-                last_leg(h, d).start()
+            def _(h=h):
+                last_leg(h, s, d).start()
 
             @pl.when(jnp.logical_not(elsewhere(relayed[d][h])))
-            def _(h=h, d=d):
-                mir_in[mine, spans[d]] = relay[d - 1, h]
-
-    def mir_arrive(d):
+            def _(h=h):
+                mir_in[mine, span(s, d)] = relay[s, d - 1, h]
+
+    order = (1, 3, 2)
+    for d in order:
+        depart(0, d)
+    depart(0, 0)
+    for s in range(SETS):
+        if s + 1 < SETS:
+            for d in order:
+                depart(s + 1, d)
+        for d in order:
+            forward(s, d)
+        if s + 1 < SETS:
+            depart(s + 1, 0)
+
+    def mir_arrive(s, d):
         for g in range(2):
             @pl.when(elsewhere(relays[d][g]))
             def _(g=g):
-                landing(g, d).wait_recv()
+                landing(g, s, d).wait_recv()
 
     def mir_leave():
-        for h in range(2):
-            @pl.when(other[h])
-            def _(h=h):
-                first_leg(h, 0).wait_send()
-
-            for d in range(1, SPREAD):
-                first_leg(h, d).wait_send()
-
-                @pl.when(elsewhere(relayed[d][h]))
-                def _(h=h, d=d):
-                    last_leg(h, d).wait_send()
+        for s in range(SETS):
+            for h in range(2):
+                @pl.when(other[h])
+                def _(h=h, s=s):
+                    direct(h, s).wait_send()
+
+                for d in order:
+                    first_leg(h, s, d).wait_send()
+
+                    @pl.when(elsewhere(relayed[d][h]))
+                    def _(h=h, s=s, d=d):
+                        last_leg(h, s, d).wait_send()
 
     tgt_arrive()
 
@@ -444,15 +488,15 @@
 
     tgt_here[...] = target[...].astype(F32)
 
-    def head(j):
+    def head(j, apart):
         mirrored = facing(mir_in[0, j].astype(F32), mir_in[1, j].astype(F32), low)
-        own = jnp.concatenate([hid[j], hid[j + half]], axis=1)
+        own = jnp.concatenate([hid[j], hid[j + apart]], axis=1)
         symmetric = (own + mirrored).astype(BF16)
         logits = jnp.dot(weight, symmetric, preferred_element_type=F32) + bias
         e = jnp.exp(logits - jnp.max(logits, axis=0, keepdims=True))
         probability = e / jnp.sum(e, axis=0, keepdims=True)
         t_own = jnp.concatenate(
-            [tgt_here[pl.ds(j, 1), :], tgt_here[pl.ds(j + half, 1), :]], axis=1
+            [tgt_here[pl.ds(j, 1), :], tgt_here[pl.ds(j + apart, 1), :]], axis=1
         )
         t_mirror = facing(tgt_in[0, pl.ds(j, 1), :], tgt_in[1, pl.ds(j, 1), :], low_row)
         grad = (probability - (bin_ids == t_own).astype(F32)).astype(BF16).astype(F32)
@@ -460,20 +504,34 @@
         bins_sum = (grad + grad_mirror).astype(BF16)
         back = jnp.dot(weight_t, bins_sum, preferred_element_type=F32)
         for n in range(2):
-            o = j + half * n
+            o = j + apart * n
             dm[HALO + o] = (back[:, tq * n : tq * (n + 1)] * slope2[o]).astype(BF16)
 
-    for d in (order[-1:] + order[:-1]):
-        mir_arrive(d)
-
-        def heads(n, carry, d=d):
-            for k in range(HEADS):
-                head(chunk * d + HEADS * n + k)
-            return carry
-
-        lax.fori_loop(0, chunk // HEADS, heads, 0)
-
-    finish_d = edges(dm, dh, 1, 8, lambda: None)
+    send_rows, fill, begin, take_rows, take, finish_d = edges(
+        dm, dh, 1, 8, [(2, blocks - 5), (0, 2), (blocks - 3, 3)]
+    )
+    for s in range(SETS):
+        apart = tp - part * (2 * s + 1)
+        for d in (0, *order):
+            mir_arrive(s, d)
+
+            def heads(n, carry, s=s, d=d, apart=apart):
+                for k in range(HEADS):
+                    head(part * s + chunk * d + HEADS * n + k, apart)
+                return carry
+
+            lax.fori_loop(0, chunk // HEADS, heads, 0)
+        if s == 0:
+            send_rows()
+            take_rows()
+            for n in (1, 2):
+                fill(n)
+                begin(n)
+
+    fill(0)
+    begin(0)
+    for n in (1, 2, 0):
+        take(n)
 
     def second_back(o, total):
         ok = row_ok(o - D1)
@@ -482,14 +540,14 @@
             delta = grad * slope1[o + D1, :, tq * n : tq * (n + 1)] * ok
             dst[o] = (delta * side_ok if n else delta).astype(BF16)
 
-    conv(w2t, wide_rows(dm, dh, D2), ext, D2, second_back)
+    conv(w2t, wide_rows(dm, dh, D2), D2, second_back, (nothing, 0, ext))
 
     def first_back(m, total):
         for n in range(2):
             o = 2 * m + n
-            out[o] = em[o + D1].astype(F32) + total[:, tq * n : tq * (n + 1)]
-
-    conv(w1t, row_pairs(em, eh, D1), (tp + 2 * D1) // 2, D1 // 2, first_back)
+            out[:, o, :] = em[o + D1].astype(F32) + total[:, tq * n : tq * (n + 1)]
+
+    conv(w1t, row_pairs(em, eh, D1), D1 // 2, first_back, (nothing, 0, (tp + 2 * D1) // 2))
 
     tgt_leave()
     finish_x()
@@ -508,7 +566,7 @@
     plane = lambda n, dtype=BF16: pltpu.VMEM((n, ch, tq), dtype)
     out = pl.pallas_call(
         functools.partial(kernel, rows, cols),
-        out_shape=jax.ShapeDtypeStruct((tp, ch, tq), F32),
+        out_shape=jax.ShapeDtypeStruct((ch, tp, tq), F32),
         in_specs=[pl.BlockSpec(memory_space=pl.ANY)] + [vmem] * 7,
         out_specs=vmem,
         scratch_shapes=[
@@ -523,14 +581,15 @@
             pltpu.VMEM((2, 2, blocks, ch, tq), BF16),
             pltpu.VMEM((2, tp // 2, ch, tq), BF16),
             pltpu.VMEM((2, tp // 2, ch, tq), BF16),
-            pltpu.VMEM((SPREAD - 1, 2, tp // 2 // SPREAD, ch, tq), BF16),
+            pltpu.VMEM((SETS, SPREAD - 1, 2, tp // 2 // SETS // SPREAD, ch, tq), BF16),
             pltpu.VMEM((2, tp // 2, tq), F32),
             pltpu.VMEM((2, tp // 2, tq), F32),
             pltpu.VMEM((tp, tq), F32),
             pltpu.SemaphoreType.DMA((18,)),
             pltpu.SemaphoreType.DMA((18,)),
             pltpu.SemaphoreType.DMA((1,)),
-            *[pltpu.SemaphoreType.DMA((2, SPREAD))] * 4,
+            *[pltpu.SemaphoreType.DMA((SETS, 2, SPREAD))] * 4,
+            pltpu.VMEM((ch, tp, tq), BF16),
             pltpu.VMEM((128, 128), F32),
             pltpu.VMEM((-(-head_weight.shape[0] // 8) * 8, tq), F32),
             *[pltpu.VMEM((ext // 4 , 2 * ch, 2 * tq), F32) for n in range(8)],
@@ -539,11 +598,11 @@
             collective_id=0, has_side_effects=True, vmem_limit_bytes=60 * 1024 * 1024
         ),
     )(
-        jnp.transpose(pair_features, (1, 0, 2)),
+        pair_features,
         first_kernel, second_kernel, first_bias[None], second_bias[None],
         head_weight, head_bias[None], target,
     )
-    return jnp.transpose(out, (1, 0, 2))
+    return out
 
 
 def solution(mesh):

time: 167 us -> 149 us (0.89)
  the two profiles are of different devices: /device:TPU:57 before, /device:TPU:27 now
where the time goes in v3:
time: 149 us
  Pallas kernels  146 us (98%)
  local copies, waits for them, and re-layouts  3.16 us (2%)
    pallas_call x1, Pallas kernels, local_step(): pl.pallas_call(functools.partial(kernel, rows, cols), out_shape=jax.Shape...  146 us
    unnamed x1, local copies, waits for them, and re-layouts  3.16 us

profile of v3, /device:TPU:27, one launch (start us, length us, event | category | flops | bytes accessed | tf_op | source)
XLA Modules:
  0.0 149.1 jit_solution(14752141383709005563)
XLA Ops:
  0.0 146.0 %shard_map.82 = f32[64,64,128]{2,1,0:T(8,128)} custom-call(bf16[64,64,128]{2,1,0:T(8,128)(2,1)} %x_hbm.1, bf16[3,3,64,64]{3,2,1,0:T(8,128)(2,1)} %k1.1, bf16[3,3,64,64]{3,2,1,0:T(8,128)(2,1)} %k2.1, f32[1,64]{1,0:T(1,128)} %bitcast.3, f32[1,64]{1,0:T(1,128)} %bitcast.4, bf16[37,64]{1,0:T(8,128)(2,1)} %hw.1, f32[1,37]{1,0:T(1,128)} %bitcast.5, s32[64,128]{1,0:T(8,128)} %target.1), custom_call_target="tpu_custom_call" | custom-call | tf_op jit(solution)/shard_map/pallas_call | solution.py:567
  146.0 3.2 %copy.10 = f32[64,64,128]{2,1,0:T(8,128)} copy(f32[64,64,128]{2,1,0:T(8,128)} %shard_map.82) | data formatting | bytes 4194304

commit v4 on v3

--- a/solution.py
+++ b/solution.py
@@ -13,6 +13,7 @@
 PER = 128 // HALO
 SPREAD = 4
 SETS = 2
+UNROLL = 4
 HEADS = 2
 MESH = pl.DeviceIdType.MESH
 F32, BF16 = jnp.float32, jnp.bfloat16
@@ -241,7 +242,7 @@
     def conv(weights, patches, lag, done, *ranges):
         w = weights[...]
 
-        unroll = 4
+        unroll = UNROLL
 
         def body(b, finish):
             ys = []
@@ -530,9 +531,6 @@
 
     fill(0)
     begin(0)
-    for n in (1, 2, 0):
-        take(n)
-
     def second_back(o, total):
         ok = row_ok(o - D1)
         for n, (src, dst) in enumerate(((dm, em), (dh, eh))):
@@ -540,7 +538,12 @@
             delta = grad * slope1[o + D1, :, tq * n : tq * (n + 1)] * ok
             dst[o] = (delta * side_ok if n else delta).astype(BF16)
 
-    conv(w2t, wide_rows(dm, dh, D2), D2, second_back, (nothing, 0, ext))
+    inner, outer = 2 * PER, (blocks - 3) * PER
+    conv(
+        w2t, wide_rows(dm, dh, D2), D2, second_back,
+        (corners, 0, inner), (nothing, outer, ext),
+        (lambda: take(0), inner - 2 * D2, outer + 2 * D2),
+    )
 
     def first_back(m, total):
         for n in range(2):
@@ -592,7 +595,7 @@
             pltpu.VMEM((ch, tp, tq), BF16),
             pltpu.VMEM((128, 128), F32),
             pltpu.VMEM((-(-head_weight.shape[0] // 8) * 8, tq), F32),
-            *[pltpu.VMEM((ext // 4 , 2 * ch, 2 * tq), F32) for n in range(8)],
+            *[pltpu.VMEM((ext // UNROLL, 2 * ch, 2 * tq), F32)] * UNROLL,
         ],
         compiler_params=pltpu.CompilerParams(
             collective_id=0, has_side_effects=True, vmem_limit_bytes=60 * 1024 * 1024

time: 149 us -> 148 us (level)
  no operation moved by 1% of the time
where the time goes in v4:
time: 148 us
  Pallas kernels  145 us (98%)
  local copies, waits for them, and re-layouts  3.16 us (2%)
    pallas_call x1, Pallas kernels, local_step(): pl.pallas_call(functools.partial(kernel, rows, cols), out_shape=jax.Shape...  145 us
    unnamed x1, local copies, waits for them, and re-layouts  3.16 us

profile of v4, /device:TPU:27, one launch (start us, length us, event | category | flops | bytes accessed | tf_op | source)
XLA Modules:
  0.0 147.7 jit_solution(174905697690730865)
XLA Ops:
  0.0 144.5 %shard_map.82 = f32[64,64,128]{2,1,0:T(8,128)} custom-call(bf16[64,64,128]{2,1,0:T(8,128)(2,1)} %x_hbm.1, bf16[3,3,64,64]{3,2,1,0:T(8,128)(2,1)} %k1.1, bf16[3,3,64,64]{3,2,1,0:T(8,128)(2,1)} %k2.1, f32[1,64]{1,0:T(1,128)} %bitcast.3, f32[1,64]{1,0:T(1,128)} %bitcast.4, bf16[37,64]{1,0:T(8,128)(2,1)} %hw.1, f32[1,37]{1,0:T(1,128)} %bitcast.5, s32[64,128]{1,0:T(8,128)} %target.1), custom_call_target="tpu_custom_call" | custom-call | tf_op jit(solution)/shard_map/pallas_call | solution.py:570
  144.6 3.2 %copy.10 = f32[64,64,128]{2,1,0:T(8,128)} copy(f32[64,64,128]{2,1,0:T(8,128)} %shard_map.82) | data formatting | bytes 4194304
